TPU v7x, 768 devices: a whole 4x8x12 slice. The times are simulated.
768 devices in a mesh: row: 96 (over x, z, core), col: 8 (over y).
Axes of the slice: x: 4, y: 8, z: 12, core: 2. Of those that a mesh axis runs over, the one named last changes fastest.
Arguments:
- obs_resid: float32 [96, 32768], P('row', 'col'), may hold values from -6 to 6
- obs_cell: int32 [96, 32768], P('row', 'col'), may hold values from 0 to 66559
- azimuth: float32 [96, 32768], P('row', 'col'), may hold values from -3.140625 to 3.140625
- gate_count: int32 [96, 8], P('row', 'col'), may hold values from 1024 to 4096, as said below
- kappa_xx: float32 [65, 768, 1024], P(None, 'row', 'col'), may hold values from 0.1 to 0.2
- kappa_yy: float32 [65, 768, 1024], P(None, 'row', 'col'), may hold values from 0.1 to 0.2
- kappa_shear: float32 [65, 768, 1024], P(None, 'row', 'col'), may hold values from -0.24 to 0.24
- norm_scale: float32 [2, 65, 768, 1024], P(None, None, 'row', 'col'), may hold values from 0.5 to 2
Outputs:
- control_grad: float32 [2, 65, 768, 1024], P(None, None, 'row', 'col')
Inputs may be any that keep to these rules, and one draw needn't show every extreme that they name: `gate_count`: some tile has all 4096 slots live.
All inputs are finite; a program needn't handle non-finite values.
Results may differ from a plain program's by a relative error of at most 0.00002.
Values sent between devices are 32-bit elements; how exact they have to be, the bound alone decides.
No kernel may reach another device: no remote copies, remote signals or barrier semaphores. Data moves between devices by JAX's collectives and lax.ppermute only.
A program may use at most 32 MiB of HBM per device.

v0:
```python
import jax
import jax.numpy as jnp
from jax import lax
from jax.sharding import PartitionSpec as P

STEPS = 4


def padded_2(array, sides, width):
    for axis, dim in sides:
        size, length = (lax.axis_size(axis), array.shape[dim])
        up = [(i, (i + 1) % size) for i in range(size - 1)]
        down = [(j, i) for i, j in up]
        last = lax.slice_in_dim(array, length - width, length, axis=dim)
        leading = lax.slice_in_dim(array, 0, width, axis=dim)
        before = lax.ppermute(last, axis, up)
        after = lax.ppermute(leading, axis, down)
        array = jnp.concatenate([before, array, after], axis=dim)
    return array


def shifted(array, axis, by):
    length = lax.axis_size(axis)
    pairs = [(i, i + by) for i in range(length) if 0 <= i + by < length]
    return lax.ppermute(array, axis, pairs)


def relax(field, kappa):
    coef_xx = kappa[0, :, :-1, :-1]
    coef_xy = kappa[1, :, :-1, :-1]
    coef_yy = kappa[2, :, :-1, :-1]
    grad_x = field[..., :-1, 1:] - field[..., :-1, :-1]
    grad_y = field[..., 1:, :-1] - field[..., :-1, :-1]
    flux_x = coef_xx * grad_x + coef_xy * grad_y
    flux_y = coef_xy * grad_x + coef_yy * grad_y
    spread = flux_x[..., 1:, :-1] - flux_x[..., 1:, 1:] + flux_y[..., :-1, 1:] - flux_y[..., 1:, 1:]
    return field[..., 1:-1, 1:-1] - spread


def on_device(
    obs_resid, obs_cell, azimuth, gate_count, kappa_xx, kappa_yy, kappa_shear, norm_scale
):
    levels, rows, cols = kappa_xx.shape
    slots = obs_resid.shape[1]
    live = jnp.arange(slots, dtype=jnp.int32)[None, :] < gate_count
    weight = jnp.where(live, obs_resid, jnp.zeros_like(obs_resid)).reshape(-1)
    target = obs_cell.reshape(-1)
    angles = azimuth.reshape(-1)
    count = levels * rows * cols
    wind_u = jax.ops.segment_sum(weight * jnp.sin(angles), target, num_segments=count)
    wind_v = jax.ops.segment_sum(weight * jnp.cos(angles), target, num_segments=count)
    wind = jnp.stack([wind_u, wind_v]).reshape(2, levels, rows, cols)
    padded = padded_2(wind, (("row", 2), ("col", 3)), 1)
    along_y = 0.5 * (padded[..., 2:, 1:-1] - padded[..., :-2, 1:-1])
    along_x = 0.5 * (padded[..., 1:-1, 2:] - padded[..., 1:-1, :-2])
    field = jnp.stack([along_y[0] - along_x[1], -along_x[0] - along_y[1]])
    kappa = jnp.stack([kappa_xx, kappa_shear * jnp.sqrt(kappa_xx * kappa_yy), kappa_yy])
    lower_row = shifted(kappa[:, :, rows - 1 :, :], "row", 1)
    left_column = shifted(kappa[:, :, :, cols - 1 :], "col", 1)
    corner = jnp.zeros((3, levels, 1, 1), jnp.float32)
    top_edge = jnp.concatenate([corner, lower_row], axis=3)
    main_part = jnp.concatenate([left_column, kappa], axis=3)
    kappa_low = jnp.concatenate([top_edge, main_part], axis=2)
    kappa_wide = jnp.pad(kappa_low, ((0, 0), (0, 0), (0, 1), (0, 1)))

    def single(index, current):
        widened = padded_2(current, (("row", 2), ("col", 3)), 1)
        return relax(widened, kappa_wide)

    field = lax.fori_loop(0, STEPS, single, field)
    return norm_scale * field


def solution(mesh):
    in_specs = (
        P("row", "col"),
        P("row", "col"),
        P("row", "col"),
        P("row", "col"),
        P(None, "row", "col"),
        P(None, "row", "col"),
        P(None, "row", "col"),
        P(None, None, "row", "col"),
    )
    out_specs = P(None, None, "row", "col")
    return jax.shard_map(
        on_device, mesh=mesh, in_specs=in_specs, out_specs=out_specs, check_vma=False
    )
```

profile of v0, /device:TPU:62, one launch (start us, length us, event | category | flops | bytes accessed | tf_op | source)
XLA Modules:
  0.0 209.3 jit_solution(8465292922717937893)
XLA Ops:
  0.7 1.2 sine_multiply_fusion
  2.0 22.1 %scatter_custom_fusion.1 = f32[66560]{0:T(1024)S(1)} fusion(s32[4096]{0:T(1024)} %bitcast.33, f32[4096]{0:T(1024)S(1)} %bitcast.32, f32[]{:T(128)} %constant.2.clone.1), kind=kCustom, calls=%fused_computation.47 | custom fusion | flops 4096 | bytes 266752 | tf_op jit(solution)/shard_map/scatter-add | solution.py:51
  24.0 22.1 %scatter_custom_fusion = f32[66560]{0:T(1024)S(1)} fusion(s32[4096]{0:T(1024)} %bitcast.34, f32[4096]{0:T(1024)S(1)} %bitcast.31, f32[]{:T(128)} %constant.2.clone.1), kind=kCustom, calls=%fused_computation.49 | custom fusion | flops 4096 | bytes 266752 | tf_op jit(solution)/shard_map/scatter-add | solution.py:50
  46.2 14.3 %collective-permute-start.4 = (f32[2,65,1,128]{3,2,1,0:T(1,128)S(1)}, f32[2,65,1,128]{3,2,1,0:T(1,128)S(1)}, u32[]{:S(2)}, u32[]{:S(2)}) collective-permute-start(f32[2,65,1,128]{3,2,1,0:T(1,128)S(1)} %get-tuple-element.53), channel_id=1, source_target_pairs={{8,0},{16,8},{24,16},{32,24},{40,32},{48,40},{56,48},{64,56},{72,6... | collective-permute-start | bytes 199688 | tf_op jit(solution)/shard_map/ppermute | solution.py:17
  60.5 1.9 collective-permute-start.5
  63.2 1.3 collective-permute-start.9
  64.5 3.7 %collective-permute-done.5 = f32[2,65,1,128]{3,2,1,0:T(1,128)S(1)} collective-permute-done((f32[2,65,1,128]{3,2,1,0:T(1,128)S(1)}, f32[2,65,1,128]{3,2,1,0:T(1,128)S(1)}, u32[]{:S(2)}, u32[]{:S(2)}) %collective-permute-start.5) | collective-permute-done | bytes 66592 | tf_op jit(solution)/shard_map/ppermute | solution.py:16
  68.2 0.6 copy-done.5
  69.4 1.0 copy.28
  70.8 1.3 collective-permute-start.7
  72.1 4.5 %collective-permute-start.6 = (f32[2,65,10,1]{1,0,3,2:T(2,128)}, f32[2,65,10,1]{1,0,3,2:T(2,128)S(1)}, u32[]{:S(2)}, u32[]{:S(2)}) collective-permute-start(f32[2,65,10,1]{1,0,3,2:T(2,128)} %copy.28), channel_id=1, source_target_pairs={{1,0},{2,1},{3,2},{4,3},{5,4},{6,5},{7,6},{9,8},{10,9},{11,10},{12... | collective-permute-start | bytes 15608 | tf_op jit(solution)/shard_map/ppermute | solution.py:17
  76.6 0.7 pad_maximum_fusion.18
  77.4 2.1 collective-permute-start.8
  79.5 1.3 copy.33
  80.8 0.6 copy.29
  81.3 1.2 copy.31
  82.6 1.9 fusion.5
  85.2 0.6 collective-permute-done.8
  85.7 3.8 %select_maximum_fusion = f32[3,65,9,129]{3,2,1,0:T(8,128)} fusion(f32[3,65,1,128]{3,2,1,0:T(1,128)} %collective-permute-done.8, f32[1,65,8,128]{3,2,1,0:T(8,128)S(1)} %bitcast.27, f32[1,65,8,128]{3,2,1,0:T(8,128)S(1)} %multiply_bitcast_fusion, f32[1,65,8,128]{3,2,1,0:T(8,128)S(1)} %bitcast.30, f32[3,65,8,1]{3,2,1,0:T(8,128)S(1)} %copy-done.3), kind=kLoop, calls=%fused_computation.21 | loop fusion | flops 1358370 | bytes 1810380 | tf_op jit(solution)/shard_map/concatenate | solution.py:63
  89.6 4.5 %copy.37 = f32[3,65,9,129]{1,3,2,0:T(8,128)} copy(f32[3,65,9,129]{3,2,1,0:T(8,128)} %select_maximum_fusion) | data formatting | bytes 1811160
  94.1 1.6 pad.5.clone
  95.7 111.7 %while.10 = (s32[]{:T(128)}, f32[2,65,8,128]{1,0,3,2:T(2,128)S(1)}, f32[3,65,10,130]{1,3,2,0:T(8,128)S(1)}, s32[]{:T(128)}) while((s32[]{:T(128)}, f32[2,65,8,128]{1,0,3,2:T(2,128)S(1)}, f32[3,65,10,130]{1,3,2,0:T(8,128)S(1)}, s32[]{:T(128)}) %tuple.39), condition=%wide.region_3.4_spmd, body=%wide.region_2.3_spmd.sunk | while | flops 2645502 | bytes 13875749 | solution.py:70
  95.8 1.9 collective-permute-start
  97.7 5.8 %collective-permute-start.1 = (f32[2,65,1,128]{1,0,3,2:T(2,128)S(1)}, f32[2,65,1,128]{1,0,3,2:T(2,128)S(1)}, u32[]{:S(2)}, u32[]{:S(2)}) collective-permute-start(f32[2,65,1,128]{1,0,3,2:T(2,128)S(1)} %get-tuple-element.88), channel_id=1, source_target_pairs={{8,0},{16,8},{24,16},{32,24},{40,32},{48,40},{56,48},{64,56},{72,6... | collective-permute-start | bytes 199688 | tf_op jit(solution)/shard_map/while/body/eval_jaxpr/ppermute | solution.py:17
  103.5 0.7 collective-permute-done
  104.3 1.6 collective-permute-done.1
  106.0 3.3 %collective-permute-start.2 = (f32[2,65,10,1]{1,0,3,2:T(2,128)S(1)}, f32[2,65,10,1]{1,0,3,2:T(2,128)S(1)}, u32[]{:S(2)}, u32[]{:S(2)}) collective-permute-start(f32[2,65,10,1]{1,0,3,2:T(2,128)S(1)} %get-tuple-element.89), channel_id=1, source_target_pairs={{1,0},{2,1},{3,2},{4,3},{5,4},{6,5},{7,6},{9,8},{10,9},{11,10},{12... | collective-permute-start | bytes 15608 | tf_op jit(solution)/shard_map/while/body/eval_jaxpr/ppermute | solution.py:17
  109.3 1.3 collective-permute-start.3
  110.6 1.3 slice_bitcast_fusion.4
  111.9 2.9 %collective-permute-done.3 = f32[2,65,10,1]{1,0,3,2:T(2,128)S(1)} collective-permute-done((f32[2,65,10,1]{1,0,3,2:T(2,128)S(1)}, f32[2,65,10,1]{1,0,3,2:T(2,128)S(1)}, u32[]{:S(2)}, u32[]{:S(2)}) %collective-permute-start.3) | collective-permute-done | bytes 5232 | tf_op jit(solution)/shard_map/while/body/eval_jaxpr/ppermute | solution.py:16
  114.9 6.8 %multiply_add_fusion.3 = (f32[2,65,9,129]{1,0,3,2:T(2,128)S(1)}, f32[2,65,9,129]{1,0,3,2:T(2,128)S(1)}) fusion(f32[65,9,129]{0,2,1:T(8,128)} %get-tuple-element.85, f32[65,9,129]{0,2,1:T(8,128)} %get-tuple-element.86, f32[2,65,10,1]{1,0,3,2:T(2,128)S(1)} %collective-permute-done.2, f32[2,65,10,128]{1,0,3,2:T(2,128)} %copy-done, ...), kind=kLoop, calls=%fused_computation.10.clone.1 | loop fusion | flops 2113020 | bytes 2789020 | tf_op jit(solution)/shard_map/while/body/eval_jaxpr/add | solution.py:34
  121.6 1.5 fusion.20
  123.2 1.9 collective-permute-start
  125.1 5.8 %collective-permute-start.1 = (f32[2,65,1,128]{1,0,3,2:T(2,128)S(1)}, f32[2,65,1,128]{1,0,3,2:T(2,128)S(1)}, u32[]{:S(2)}, u32[]{:S(2)}) collective-permute-start(f32[2,65,1,128]{1,0,3,2:T(2,128)S(1)} %get-tuple-element.88), channel_id=1, source_target_pairs={{8,0},{16,8},{24,16},{32,24},{40,32},{48,40},{56,48},{64,56},{72,6... | collective-permute-start | bytes 199688 | tf_op jit(solution)/shard_map/while/body/eval_jaxpr/ppermute | solution.py:17
  130.9 0.7 collective-permute-done
  131.8 1.6 collective-permute-done.1
  133.4 3.8 %collective-permute-start.2 = (f32[2,65,10,1]{1,0,3,2:T(2,128)S(1)}, f32[2,65,10,1]{1,0,3,2:T(2,128)S(1)}, u32[]{:S(2)}, u32[]{:S(2)}) collective-permute-start(f32[2,65,10,1]{1,0,3,2:T(2,128)S(1)} %get-tuple-element.89), channel_id=1, source_target_pairs={{1,0},{2,1},{3,2},{4,3},{5,4},{6,5},{7,6},{9,8},{10,9},{11,10},{12... | collective-permute-start | bytes 15608 | tf_op jit(solution)/shard_map/while/body/eval_jaxpr/ppermute | solution.py:17
  137.2 1.3 collective-permute-start.3
  138.5 1.3 slice_bitcast_fusion.4
  139.9 2.9 %collective-permute-done.3 = f32[2,65,10,1]{1,0,3,2:T(2,128)S(1)} collective-permute-done((f32[2,65,10,1]{1,0,3,2:T(2,128)S(1)}, f32[2,65,10,1]{1,0,3,2:T(2,128)S(1)}, u32[]{:S(2)}, u32[]{:S(2)}) %collective-permute-start.3) | collective-permute-done | bytes 5232 | tf_op jit(solution)/shard_map/while/body/eval_jaxpr/ppermute | solution.py:16
  142.8 6.8 %multiply_add_fusion.3 = (f32[2,65,9,129]{1,0,3,2:T(2,128)S(1)}, f32[2,65,9,129]{1,0,3,2:T(2,128)S(1)}) fusion(f32[65,9,129]{0,2,1:T(8,128)} %get-tuple-element.85, f32[65,9,129]{0,2,1:T(8,128)} %get-tuple-element.86, f32[2,65,10,1]{1,0,3,2:T(2,128)S(1)} %collective-permute-done.2, f32[2,65,10,128]{1,0,3,2:T(2,128)} %copy-done, ...), kind=kLoop, calls=%fused_computation.10.clone.1 | loop fusion | flops 2113020 | bytes 2789020 | tf_op jit(solution)/shard_map/while/body/eval_jaxpr/add | solution.py:34
  149.6 1.5 fusion.20
  151.2 1.9 collective-permute-start
  153.1 5.8 %collective-permute-start.1 = (f32[2,65,1,128]{1,0,3,2:T(2,128)S(1)}, f32[2,65,1,128]{1,0,3,2:T(2,128)S(1)}, u32[]{:S(2)}, u32[]{:S(2)}) collective-permute-start(f32[2,65,1,128]{1,0,3,2:T(2,128)S(1)} %get-tuple-element.88), channel_id=1, source_target_pairs={{8,0},{16,8},{24,16},{32,24},{40,32},{48,40},{56,48},{64,56},{72,6... | collective-permute-start | bytes 199688 | tf_op jit(solution)/shard_map/while/body/eval_jaxpr/ppermute | solution.py:17
  158.8 0.7 collective-permute-done
  159.7 1.6 collective-permute-done.1
  161.4 4.1 %collective-permute-start.2 = (f32[2,65,10,1]{1,0,3,2:T(2,128)S(1)}, f32[2,65,10,1]{1,0,3,2:T(2,128)S(1)}, u32[]{:S(2)}, u32[]{:S(2)}) collective-permute-start(f32[2,65,10,1]{1,0,3,2:T(2,128)S(1)} %get-tuple-element.89), channel_id=1, source_target_pairs={{1,0},{2,1},{3,2},{4,3},{5,4},{6,5},{7,6},{9,8},{10,9},{11,10},{12... | collective-permute-start | bytes 15608 | tf_op jit(solution)/shard_map/while/body/eval_jaxpr/ppermute | solution.py:17
  165.5 1.3 collective-permute-start.3
  166.8 1.3 slice_bitcast_fusion.4
  168.1 2.9 %collective-permute-done.3 = f32[2,65,10,1]{1,0,3,2:T(2,128)S(1)} collective-permute-done((f32[2,65,10,1]{1,0,3,2:T(2,128)S(1)}, f32[2,65,10,1]{1,0,3,2:T(2,128)S(1)}, u32[]{:S(2)}, u32[]{:S(2)}) %collective-permute-start.3) | collective-permute-done | bytes 5232 | tf_op jit(solution)/shard_map/while/body/eval_jaxpr/ppermute | solution.py:16
  171.0 6.8 %multiply_add_fusion.3 = (f32[2,65,9,129]{1,0,3,2:T(2,128)S(1)}, f32[2,65,9,129]{1,0,3,2:T(2,128)S(1)}) fusion(f32[65,9,129]{0,2,1:T(8,128)} %get-tuple-element.85, f32[65,9,129]{0,2,1:T(8,128)} %get-tuple-element.86, f32[2,65,10,1]{1,0,3,2:T(2,128)S(1)} %collective-permute-done.2, f32[2,65,10,128]{1,0,3,2:T(2,128)} %copy-done, ...), kind=kLoop, calls=%fused_computation.10.clone.1 | loop fusion | flops 2113020 | bytes 2789020 | tf_op jit(solution)/shard_map/while/body/eval_jaxpr/add | solution.py:34
  177.8 1.5 fusion.20
  179.4 1.9 collective-permute-start
  181.3 5.8 %collective-permute-start.1 = (f32[2,65,1,128]{1,0,3,2:T(2,128)S(1)}, f32[2,65,1,128]{1,0,3,2:T(2,128)S(1)}, u32[]{:S(2)}, u32[]{:S(2)}) collective-permute-start(f32[2,65,1,128]{1,0,3,2:T(2,128)S(1)} %get-tuple-element.88), channel_id=1, source_target_pairs={{8,0},{16,8},{24,16},{32,24},{40,32},{48,40},{56,48},{64,56},{72,6... | collective-permute-start | bytes 199688 | tf_op jit(solution)/shard_map/while/body/eval_jaxpr/ppermute | solution.py:17
  187.1 0.7 collective-permute-done
  187.9 1.6 collective-permute-done.1
  189.6 3.9 %collective-permute-start.2 = (f32[2,65,10,1]{1,0,3,2:T(2,128)S(1)}, f32[2,65,10,1]{1,0,3,2:T(2,128)S(1)}, u32[]{:S(2)}, u32[]{:S(2)}) collective-permute-start(f32[2,65,10,1]{1,0,3,2:T(2,128)S(1)} %get-tuple-element.89), channel_id=1, source_target_pairs={{1,0},{2,1},{3,2},{4,3},{5,4},{6,5},{7,6},{9,8},{10,9},{11,10},{12... | collective-permute-start | bytes 15608 | tf_op jit(solution)/shard_map/while/body/eval_jaxpr/ppermute | solution.py:17
  193.5 1.3 collective-permute-start.3
  194.8 1.3 slice_bitcast_fusion.4
  196.2 2.9 %collective-permute-done.3 = f32[2,65,10,1]{1,0,3,2:T(2,128)S(1)} collective-permute-done((f32[2,65,10,1]{1,0,3,2:T(2,128)S(1)}, f32[2,65,10,1]{1,0,3,2:T(2,128)S(1)}, u32[]{:S(2)}, u32[]{:S(2)}) %collective-permute-start.3) | collective-permute-done | bytes 5232 | tf_op jit(solution)/shard_map/while/body/eval_jaxpr/ppermute | solution.py:16
  199.1 6.8 %multiply_add_fusion.3 = (f32[2,65,9,129]{1,0,3,2:T(2,128)S(1)}, f32[2,65,9,129]{1,0,3,2:T(2,128)S(1)}) fusion(f32[65,9,129]{0,2,1:T(8,128)} %get-tuple-element.85, f32[65,9,129]{0,2,1:T(8,128)} %get-tuple-element.86, f32[2,65,10,1]{1,0,3,2:T(2,128)S(1)} %collective-permute-done.2, f32[2,65,10,128]{1,0,3,2:T(2,128)} %copy-done, ...), kind=kLoop, calls=%fused_computation.10.clone.1 | loop fusion | flops 2113020 | bytes 2789020 | tf_op jit(solution)/shard_map/while/body/eval_jaxpr/add | solution.py:34
  205.9 1.5 fusion.20
  207.8 0.6 copy-done.4
  208.5 0.9 mul.71
  (57 shorter events, 3.6 us)
Async XLA Ops:
  0.0 62.5 %copy-start.1 = (f32[65,8,128]{2,1,0:T(8,128)S(1)}, f32[65,8,128]{2,1,0:T(8,128)}, u32[]{:S(2)}) copy-start(f32[65,8,128]{2,1,0:T(8,128)} %param.15) | copy-start | bytes 798724
  0.0 62.5 %copy-start.2 = (f32[65,8,128]{2,1,0:T(8,128)S(1)}, f32[65,8,128]{2,1,0:T(8,128)}, u32[]{:S(2)}) copy-start(f32[65,8,128]{2,1,0:T(8,128)} %param.14) | copy-start | bytes 798724
  0.0 62.5 %copy-start.6 = (f32[65,8,128]{2,1,0:T(8,128)S(1)}, f32[65,8,128]{2,1,0:T(8,128)}, u32[]{:S(2)}) copy-start(f32[65,8,128]{2,1,0:T(8,128)} %param.16) | copy-start | bytes 798724
  46.2 18.3 %collective-permute-start.4 = (f32[2,65,1,128]{3,2,1,0:T(1,128)S(1)}, f32[2,65,1,128]{3,2,1,0:T(1,128)S(1)}, u32[]{:S(2)}, u32[]{:S(2)}) collective-permute-start(f32[2,65,1,128]{3,2,1,0:T(1,128)S(1)} %get-tuple-element.53), channel_id=1, source_target_pairs={{8,0},{16,8},{24,16},{32,24},{40,32},{48,40},{56,48},{64,56},{72,6... | collective-permute-start | bytes 199688 | tf_op jit(solution)/shard_map/ppermute | solution.py:17
  60.5 7.7 %collective-permute-start.5 = (f32[2,65,1,128]{3,2,1,0:T(1,128)S(1)}, f32[2,65,1,128]{3,2,1,0:T(1,128)S(1)}, u32[]{:S(2)}, u32[]{:S(2)}) collective-permute-start(f32[2,65,1,128]{3,2,1,0:T(1,128)S(1)} %get-tuple-element.54), channel_id=1, source_target_pairs={{0,8},{8,16},{16,24},{24,32},{32,40},{40,48},{48,56},{56,64},{64,7... | collective-permute-start | bytes 199688 | tf_op jit(solution)/shard_map/ppermute | solution.py:16
  63.2 16.3 %collective-permute-start.9 = (f32[3,65,8,1]{1,2,3,0:T(8,128)S(1)}, f32[3,65,8,1]{1,2,3,0:T(8,128)S(1)}, u32[]{:S(2)}, u32[]{:S(2)}) collective-permute-start(f32[3,65,8,1]{1,2,3,0:T(8,128)S(1)} %copy.32), channel_id=1, source_target_pairs={{0,1},{1,2},{2,3},{3,4},{4,5},{5,6},{6,7},{8,9},{9,10},{10,11},{11... | collective-permute-start | bytes 18728 | tf_op jit(solution)/shard_map/ppermute | solution.py:25
  68.2 0.6 copy-start.5
  70.8 10.5 %collective-permute-start.7 = (f32[2,65,10,1]{1,0,3,2:T(2,128)S(1)}, f32[2,65,10,1]{1,0,3,2:T(2,128)}, u32[]{:S(2)}, u32[]{:S(2)}) collective-permute-start(f32[2,65,10,1]{1,0,3,2:T(2,128)S(1)} %copy.30), channel_id=1, source_target_pairs={{0,1},{1,2},{2,3},{3,4},{4,5},{5,6},{6,7},{8,9},{9,10},{10,11},{11... | collective-permute-start | bytes 15608 | tf_op jit(solution)/shard_map/ppermute | solution.py:16
  72.1 8.7 %collective-permute-start.6 = (f32[2,65,10,1]{1,0,3,2:T(2,128)}, f32[2,65,10,1]{1,0,3,2:T(2,128)S(1)}, u32[]{:S(2)}, u32[]{:S(2)}) collective-permute-start(f32[2,65,10,1]{1,0,3,2:T(2,128)} %copy.28), channel_id=1, source_target_pairs={{1,0},{2,1},{3,2},{4,3},{5,4},{6,5},{7,6},{9,8},{10,9},{11,10},{12... | collective-permute-start | bytes 15608 | tf_op jit(solution)/shard_map/ppermute | solution.py:17
  77.4 8.4 %collective-permute-start.8 = (f32[3,65,1,128]{3,2,1,0:T(1,128)}, f32[3,65,1,128]{3,2,1,0:T(1,128)}, u32[]{:S(2)}, u32[]{:S(2)}) collective-permute-start(f32[3,65,1,128]{3,2,1,0:T(1,128)} %pad_maximum_fusion.18), channel_id=1, source_target_pairs={{0,8},{8,16},{16,24},{24,32},{32,40},{40,48},{48,56},{56,64},{64,7... | collective-permute-start | bytes 299528 | tf_op jit(solution)/shard_map/ppermute | solution.py:25
  84.6 1.1 copy-start.3
  95.8 8.4 %collective-permute-start = (f32[2,65,1,128]{1,0,3,2:T(2,128)S(1)}, f32[2,65,1,128]{1,0,3,2:T(2,128)S(1)}, u32[]{:S(2)}, u32[]{:S(2)}) collective-permute-start(f32[2,65,1,128]{1,0,3,2:T(2,128)S(1)} %get-tuple-element.87), channel_id=1, source_target_pairs={{0,8},{8,16},{16,24},{24,32},{32,40},{40,48},{48,56},{56,64},{64,7... | collective-permute-start | bytes 199688 | tf_op jit(solution)/shard_map/while/body/eval_jaxpr/ppermute | solution.py:16
  97.7 8.3 %collective-permute-start.1 = (f32[2,65,1,128]{1,0,3,2:T(2,128)S(1)}, f32[2,65,1,128]{1,0,3,2:T(2,128)S(1)}, u32[]{:S(2)}, u32[]{:S(2)}) collective-permute-start(f32[2,65,1,128]{1,0,3,2:T(2,128)S(1)} %get-tuple-element.88), channel_id=1, source_target_pairs={{8,0},{16,8},{24,16},{32,24},{40,32},{48,40},{56,48},{64,56},{72,6... | collective-permute-start | bytes 199688 | tf_op jit(solution)/shard_map/while/body/eval_jaxpr/ppermute | solution.py:17
  106.0 5.9 %copy-start = (f32[2,65,10,128]{1,0,3,2:T(2,128)}, f32[2,65,10,128]{1,0,3,2:T(2,128)S(1)}, u32[]{:S(2)}) copy-start(f32[2,65,10,128]{1,0,3,2:T(2,128)S(1)} %constant_dynamic-update-slice_fusion.8) | copy-start | bytes 1996804 | tf_op jit(solution)/shard_map/while
  106.0 5.9 %collective-permute-start.2 = (f32[2,65,10,1]{1,0,3,2:T(2,128)S(1)}, f32[2,65,10,1]{1,0,3,2:T(2,128)S(1)}, u32[]{:S(2)}, u32[]{:S(2)}) collective-permute-start(f32[2,65,10,1]{1,0,3,2:T(2,128)S(1)} %get-tuple-element.89), channel_id=1, source_target_pairs={{1,0},{2,1},{3,2},{4,3},{5,4},{6,5},{7,6},{9,8},{10,9},{11,10},{12... | collective-permute-start | bytes 15608 | tf_op jit(solution)/shard_map/while/body/eval_jaxpr/ppermute | solution.py:17
  109.3 5.6 %collective-permute-start.3 = (f32[2,65,10,1]{1,0,3,2:T(2,128)S(1)}, f32[2,65,10,1]{1,0,3,2:T(2,128)S(1)}, u32[]{:S(2)}, u32[]{:S(2)}) collective-permute-start(f32[2,65,10,1]{1,0,3,2:T(2,128)S(1)} %get-tuple-element.90), channel_id=1, source_target_pairs={{0,1},{1,2},{2,3},{3,4},{4,5},{5,6},{6,7},{8,9},{9,10},{10,11},{11... | collective-permute-start | bytes 15608 | tf_op jit(solution)/shard_map/while/body/eval_jaxpr/ppermute | solution.py:16
  123.2 8.4 %collective-permute-start = (f32[2,65,1,128]{1,0,3,2:T(2,128)S(1)}, f32[2,65,1,128]{1,0,3,2:T(2,128)S(1)}, u32[]{:S(2)}, u32[]{:S(2)}) collective-permute-start(f32[2,65,1,128]{1,0,3,2:T(2,128)S(1)} %get-tuple-element.87), channel_id=1, source_target_pairs={{0,8},{8,16},{16,24},{24,32},{32,40},{40,48},{48,56},{56,64},{64,7... | collective-permute-start | bytes 199688 | tf_op jit(solution)/shard_map/while/body/eval_jaxpr/ppermute | solution.py:16
  125.1 8.3 %collective-permute-start.1 = (f32[2,65,1,128]{1,0,3,2:T(2,128)S(1)}, f32[2,65,1,128]{1,0,3,2:T(2,128)S(1)}, u32[]{:S(2)}, u32[]{:S(2)}) collective-permute-start(f32[2,65,1,128]{1,0,3,2:T(2,128)S(1)} %get-tuple-element.88), channel_id=1, source_target_pairs={{8,0},{16,8},{24,16},{32,24},{40,32},{48,40},{56,48},{64,56},{72,6... | collective-permute-start | bytes 199688 | tf_op jit(solution)/shard_map/while/body/eval_jaxpr/ppermute | solution.py:17
  133.4 6.5 %copy-start = (f32[2,65,10,128]{1,0,3,2:T(2,128)}, f32[2,65,10,128]{1,0,3,2:T(2,128)S(1)}, u32[]{:S(2)}) copy-start(f32[2,65,10,128]{1,0,3,2:T(2,128)S(1)} %constant_dynamic-update-slice_fusion.8) | copy-start | bytes 1996804 | tf_op jit(solution)/shard_map/while
  133.4 6.4 %collective-permute-start.2 = (f32[2,65,10,1]{1,0,3,2:T(2,128)S(1)}, f32[2,65,10,1]{1,0,3,2:T(2,128)S(1)}, u32[]{:S(2)}, u32[]{:S(2)}) collective-permute-start(f32[2,65,10,1]{1,0,3,2:T(2,128)S(1)} %get-tuple-element.89), channel_id=1, source_target_pairs={{1,0},{2,1},{3,2},{4,3},{5,4},{6,5},{7,6},{9,8},{10,9},{11,10},{12... | collective-permute-start | bytes 15608 | tf_op jit(solution)/shard_map/while/body/eval_jaxpr/ppermute | solution.py:17
  137.2 5.6 %collective-permute-start.3 = (f32[2,65,10,1]{1,0,3,2:T(2,128)S(1)}, f32[2,65,10,1]{1,0,3,2:T(2,128)S(1)}, u32[]{:S(2)}, u32[]{:S(2)}) collective-permute-start(f32[2,65,10,1]{1,0,3,2:T(2,128)S(1)} %get-tuple-element.90), channel_id=1, source_target_pairs={{0,1},{1,2},{2,3},{3,4},{4,5},{5,6},{6,7},{8,9},{9,10},{10,11},{11... | collective-permute-start | bytes 15608 | tf_op jit(solution)/shard_map/while/body/eval_jaxpr/ppermute | solution.py:16
  151.2 8.4 %collective-permute-start = (f32[2,65,1,128]{1,0,3,2:T(2,128)S(1)}, f32[2,65,1,128]{1,0,3,2:T(2,128)S(1)}, u32[]{:S(2)}, u32[]{:S(2)}) collective-permute-start(f32[2,65,1,128]{1,0,3,2:T(2,128)S(1)} %get-tuple-element.87), channel_id=1, source_target_pairs={{0,8},{8,16},{16,24},{24,32},{32,40},{40,48},{48,56},{56,64},{64,7... | collective-permute-start | bytes 199688 | tf_op jit(solution)/shard_map/while/body/eval_jaxpr/ppermute | solution.py:16
  153.1 8.3 %collective-permute-start.1 = (f32[2,65,1,128]{1,0,3,2:T(2,128)S(1)}, f32[2,65,1,128]{1,0,3,2:T(2,128)S(1)}, u32[]{:S(2)}, u32[]{:S(2)}) collective-permute-start(f32[2,65,1,128]{1,0,3,2:T(2,128)S(1)} %get-tuple-element.88), channel_id=1, source_target_pairs={{8,0},{16,8},{24,16},{32,24},{40,32},{48,40},{56,48},{64,56},{72,6... | collective-permute-start | bytes 199688 | tf_op jit(solution)/shard_map/while/body/eval_jaxpr/ppermute | solution.py:17
  161.4 6.7 %copy-start = (f32[2,65,10,128]{1,0,3,2:T(2,128)}, f32[2,65,10,128]{1,0,3,2:T(2,128)S(1)}, u32[]{:S(2)}) copy-start(f32[2,65,10,128]{1,0,3,2:T(2,128)S(1)} %constant_dynamic-update-slice_fusion.8) | copy-start | bytes 1996804 | tf_op jit(solution)/shard_map/while
  161.4 6.7 %collective-permute-start.2 = (f32[2,65,10,1]{1,0,3,2:T(2,128)S(1)}, f32[2,65,10,1]{1,0,3,2:T(2,128)S(1)}, u32[]{:S(2)}, u32[]{:S(2)}) collective-permute-start(f32[2,65,10,1]{1,0,3,2:T(2,128)S(1)} %get-tuple-element.89), channel_id=1, source_target_pairs={{1,0},{2,1},{3,2},{4,3},{5,4},{6,5},{7,6},{9,8},{10,9},{11,10},{12... | collective-permute-start | bytes 15608 | tf_op jit(solution)/shard_map/while/body/eval_jaxpr/ppermute | solution.py:17
  165.5 5.6 %collective-permute-start.3 = (f32[2,65,10,1]{1,0,3,2:T(2,128)S(1)}, f32[2,65,10,1]{1,0,3,2:T(2,128)S(1)}, u32[]{:S(2)}, u32[]{:S(2)}) collective-permute-start(f32[2,65,10,1]{1,0,3,2:T(2,128)S(1)} %get-tuple-element.90), channel_id=1, source_target_pairs={{0,1},{1,2},{2,3},{3,4},{4,5},{5,6},{6,7},{8,9},{9,10},{10,11},{11... | collective-permute-start | bytes 15608 | tf_op jit(solution)/shard_map/while/body/eval_jaxpr/ppermute | solution.py:16
  179.4 8.4 %collective-permute-start = (f32[2,65,1,128]{1,0,3,2:T(2,128)S(1)}, f32[2,65,1,128]{1,0,3,2:T(2,128)S(1)}, u32[]{:S(2)}, u32[]{:S(2)}) collective-permute-start(f32[2,65,1,128]{1,0,3,2:T(2,128)S(1)} %get-tuple-element.87), channel_id=1, source_target_pairs={{0,8},{8,16},{16,24},{24,32},{32,40},{40,48},{48,56},{56,64},{64,7... | collective-permute-start | bytes 199688 | tf_op jit(solution)/shard_map/while/body/eval_jaxpr/ppermute | solution.py:16
  181.3 8.3 %collective-permute-start.1 = (f32[2,65,1,128]{1,0,3,2:T(2,128)S(1)}, f32[2,65,1,128]{1,0,3,2:T(2,128)S(1)}, u32[]{:S(2)}, u32[]{:S(2)}) collective-permute-start(f32[2,65,1,128]{1,0,3,2:T(2,128)S(1)} %get-tuple-element.88), channel_id=1, source_target_pairs={{8,0},{16,8},{24,16},{32,24},{40,32},{48,40},{56,48},{64,56},{72,6... | collective-permute-start | bytes 199688 | tf_op jit(solution)/shard_map/while/body/eval_jaxpr/ppermute | solution.py:17
  189.6 6.6 %copy-start = (f32[2,65,10,128]{1,0,3,2:T(2,128)}, f32[2,65,10,128]{1,0,3,2:T(2,128)S(1)}, u32[]{:S(2)}) copy-start(f32[2,65,10,128]{1,0,3,2:T(2,128)S(1)} %constant_dynamic-update-slice_fusion.8) | copy-start | bytes 1996804 | tf_op jit(solution)/shard_map/while
  189.6 6.5 %collective-permute-start.2 = (f32[2,65,10,1]{1,0,3,2:T(2,128)S(1)}, f32[2,65,10,1]{1,0,3,2:T(2,128)S(1)}, u32[]{:S(2)}, u32[]{:S(2)}) collective-permute-start(f32[2,65,10,1]{1,0,3,2:T(2,128)S(1)} %get-tuple-element.89), channel_id=1, source_target_pairs={{1,0},{2,1},{3,2},{4,3},{5,4},{6,5},{7,6},{9,8},{10,9},{11,10},{12... | collective-permute-start | bytes 15608 | tf_op jit(solution)/shard_map/while/body/eval_jaxpr/ppermute | solution.py:17
  193.5 5.6 %collective-permute-start.3 = (f32[2,65,10,1]{1,0,3,2:T(2,128)S(1)}, f32[2,65,10,1]{1,0,3,2:T(2,128)S(1)}, u32[]{:S(2)}, u32[]{:S(2)}) collective-permute-start(f32[2,65,10,1]{1,0,3,2:T(2,128)S(1)} %get-tuple-element.90), channel_id=1, source_target_pairs={{0,1},{1,2},{2,3},{3,4},{4,5},{5,6},{6,7},{8,9},{9,10},{10,11},{11... | collective-permute-start | bytes 15608 | tf_op jit(solution)/shard_map/while/body/eval_jaxpr/ppermute | solution.py:16
  207.4 1.0 copy-start.4
where the time goes:
time: 211 us; the launch traced here: 209 us
  other arithmetic  86.7 us (41%)
  starting transfers between devices  76.3 us (36%)
  waiting for transfers between devices  25.4 us (12%)
  local copies, waits for them, and re-layouts  19.6 us (9%)
    ppermute x10, starting transfers between devices, padded_2(): after = lax.ppermute(leading, axis, down)  56.9 us
    add x4, other arithmetic, relax(): flux_x = coef_xx * grad_x + coef_xy * grad_y  27.1 us
    scatter-add x1, other arithmetic, on_device(): jax.ops.segment_sum(weight * jnp.cos(angles), target, num_segments=count)  22.1 us
    scatter-add x1, other arithmetic, on_device(): jax.ops.segment_sum(weight * jnp.sin(angles), target, num_segments=count)  22.1 us
    ppermute x10, waiting for transfers between devices, padded_2(): before = lax.ppermute(last, axis, up)  18.3 us
    ppermute x10, starting transfers between devices, padded_2(): before = lax.ppermute(last, axis, up)  16.1 us
    ppermute x10, waiting for transfers between devices, padded_2(): after = lax.ppermute(leading, axis, down)  6.54 us
    sub x4, other arithmetic, relax(): return field[..., 1:-1, 1:-1] - spread  6.03 us
  transfers between devices with their start and end apart: 22, of which 14 were waited for; matrix products, arithmetic and copies ran while one was open for 7% of the time, Pallas kernels for 0%

commit v1 on v0

v1 whole, which is shorter than its diff:
```python
import jax
import jax.numpy as jnp
from jax import lax
from jax.experimental import pallas as pl
from jax.experimental.pallas import tpu as pltpu
from jax.sharding import PartitionSpec as P

STEPS = 4
NT = 9
LV = 8 * NT
F32 = jnp.float32
BF16 = jnp.bfloat16
KC = 1024
SPLITS = 2
NQ = 81
NM = NQ // 3
VM = pl.BlockSpec(memory_space=pltpu.VMEM)
SM = pl.BlockSpec(memory_space=pltpu.SMEM)


def pairs(size, first):
    out = []
    for i in range(first, size - 1, 2):
        out += [(i, i + 1), (i + 1, i)]
    return out


def roll(x, by):
    by = by % 128
    return x if by == 0 else pltpu.roll(x, by, 1)


def at(ref, i):
    return ref[pl.ds(pl.multiple_of(i * 8, 8), 8), :]


def strided(ref, base, tile, y):
    if tile < 8:
        return ref[pl.ds(base + tile * 64 + y, 8, stride=8), :]
    row = base + 512 + y
    return jnp.broadcast_to(ref[row : row + 1, :], (8, 128))


def lanes():
    return lax.broadcasted_iota(jnp.int32, (8, 128), 1)


def sublanes():
    return lax.broadcasted_iota(jnp.int32, (8, 128), 0)


def prepare(pos, gate, resid, cell, azimuth, kxx, kyy, ksh, pay_a, pay_b, kt):
    odd = (pos[0] & 1) == 1
    slot = lax.broadcasted_iota(jnp.int32, (32, 128), 0) * 128 + lax.broadcasted_iota(
        jnp.int32, (32, 128), 1
    )
    weight = jnp.where(slot < gate[0, 0], resid[...], 0.0)
    angle = azimuth[...]
    wu = weight * jnp.sin(angle)
    wv = weight * jnp.cos(angle)
    cf = cell[...].astype(F32)
    for pay in (pay_a, pay_b):
        pay[0:32, :] = wu
        pay[32:64, :] = wv
        pay[64:96, :] = cf
    for tile in range(NT):
        rows = []
        for y in range(8):
            xx = strided(kxx, 0, tile, y)
            yy = strided(kyy, 0, tile, y)
            xy = strided(ksh, 0, tile, y) * jnp.sqrt(xx * yy)
            rows.append((xx, xy, yy))
            for q in range(3):
                start = (q * 8 + y) * LV + tile * 8
                kt[start : start + 8, :] = rows[y][q]
        for i in range(4):
            for q in range(3):
                start = 96 + (i * 3 + q) * LV + tile * 8
                low, high = rows[i][q], rows[i + 4][q]
                pay_a[start : start + 8, :] = jnp.where(odd, low, high)
                pay_b[start : start + 8, :] = jnp.where(odd, high, low)


def scatter(wu, wv, cf, shift, count, hot, val, tab, out_u, out_v, base):
    cell = cf.astype(jnp.int32)
    level = lax.shift_right_logical(cell, 10)
    y = lax.shift_right_logical(cell, 7) & 7
    tab[0:32, :] = ((y - shift) * LV + level).astype(F32)
    tab[32:64, :] = (cell & 127).astype(F32)
    for n, value in enumerate((wu, wv)):
        for s in range(SPLITS):
            top = value.astype(BF16).astype(F32)
            value = value - top
            start = 64 + (n * SPLITS + s) * 32
            tab[start : start + 32, :] = top
    rows = lax.broadcasted_iota(jnp.int32, (count, 128), 0).astype(F32)
    cols = lax.broadcasted_iota(jnp.int32, (128, 128), 0).astype(F32)
    per = KC // 128

    def chunk(c, _):
        for j in range(per):
            i = c * per + j
            span = slice(j * 128, j * 128 + 128)
            row = tab[pl.ds(i, 1), :]
            hot[0:count, span] = jnp.where(rows == row, 1.0, 0.0).astype(BF16)
            col = tab[pl.ds(32 + i, 1), :]
            hit = cols == col
            for s in range(SPLITS):
                for n in range(2):
                    part = tab[pl.ds(64 + (n * SPLITS + s) * 32 + i, 1), :]
                    val[s * 256 + n * 128 : s * 256 + n * 128 + 128, span] = jnp.where(
                        hit, part, 0.0
                    ).astype(BF16)
        total = None
        for s in range(SPLITS):
            part = lax.dot_general(
                hot[0:count, :],
                val[s * 256 : s * 256 + 256, :],
                (((1,), (1,)), ((), ())),
                preferred_element_type=F32,
            )
            total = part if total is None else total + part

        @pl.when(c == 0)
        def _():
            out_u[base : base + count, :] = total[:, 0:128]
            out_v[base : base + count, :] = total[:, 128:256]

        @pl.when(c > 0)
        def _():
            out_u[base : base + count, :] += total[:, 0:128]
            out_v[base : base + count, :] += total[:, 128:256]

        return 0

    lax.fori_loop(0, 4096 // KC, chunk, 0)


def own_wind(obs, out_u, out_v, hot, val, tab):
    scatter(
        obs[0:32, :], obs[32:64, :], obs[64:96, :], 0, 8 * LV, hot, val, tab, out_u, out_v, 0
    )


def wind_at(own, halo, row, tile):
    if 0 <= row < 8:
        return at(own, row * NT + tile)
    return at(halo, ((row + 5) if row < 0 else row - 3) * NT + tile)


def kappa_at(kt, halo, q, row, tile):
    if 0 <= row < 8:
        return at(kt, (q * 8 + row) * NT + tile)
    return at(halo, (((row + 4) if row < 0 else row - 4) * 3 + q) * NT + tile)


def edges(pos, rec_a, rec_b, u, v, kt, hu, hv, kh, sw, sk, msg_c, msg_d, hot, val, tab):
    odd = (pos[0] & 1) == 1
    north = jnp.where(odd, rec_a[0:96, :], rec_b[0:96, :])
    south = jnp.where(odd, rec_b[0:96, :], rec_a[0:96, :])
    for part, shift, base in ((north, 3, 0), (south, 0, 5 * LV)):
        scatter(
            part[0:32], part[32:64], part[64:96], shift, 5 * LV, hot, val, tab, hu, hv, base
        )
    size = 4 * 3 * LV
    kh[0:size, :] = jnp.where(odd, rec_a[96 : 96 + size, :], rec_b[96 : 96 + size, :])
    rest = 3 * 3 * LV
    kh[size : size + rest, :] = jnp.where(
        odd, rec_b[96 : 96 + rest, :], rec_a[96 : 96 + rest, :]
    )
    lane = lanes()
    left_slot = lane // 16
    right_slot = ((lane + 4) % 128) // 16
    strips = []
    for n, (own, halo) in enumerate(((u, hu), (v, hv))):
        for row in range(-5, 13):
            strips.append((sw, n * 18 + row + 5, lambda t, o=own, h=halo, r=row: wind_at(o, h, r, t)))
    for q in range(3):
        for row in range(-4, 11):
            strips.append((sk, q * 15 + row + 4, lambda t, q=q, r=row: kappa_at(kt, kh, q, r, t)))
    odd_col = (pos[1] & 1) == 1
    fifth = lane % 16
    packed = {}
    for k, (ref, index, get) in enumerate(strips):
        left = right = None
        for j in range(8):
            moved = roll(get(j), 16 * j + 6)
            left = moved if j == 0 else jnp.where(left_slot == j, moved, left)
            right = moved if j == 0 else jnp.where(right_slot == j, moved, right)
        last = roll(get(8), 6)[0:1, :]
        start = index * 24
        ref[start : start + 8, :] = left
        ref[start + 8 : start + 16, :] = right
        ref[start + 16 : start + 24, :] = jnp.broadcast_to(last, (8, 128))
        row = NM * 8 + k
        msg_c[row : row + 1, :] = last
        msg_d[row : row + 1, :] = last
        t = k % 3
        packed[t] = (roll(left, 5 * t), roll(left, 5 * t - 5))
        if t == 2:
            right_edge, left_edge = (
                jnp.where(fifth < 6, packed[0][e], jnp.where(fifth < 11, packed[1][e], packed[2][e]))
                for e in range(2)
            )
            start = (k // 3) * 8
            msg_c[start : start + 8, :] = jnp.where(odd_col, left_edge, right_edge)
            msg_d[start : start + 8, :] = jnp.where(odd_col, right_edge, left_edge)
    fill = NM * 8 + NQ
    for msg in (msg_c, msg_d):
        msg[fill : fill + 7, :] = jnp.zeros((7, 128), F32)


def diffuse(wind, kappa, low, high, mask):
    field = {}
    for row in range(-4, 12):
        side = low if row < 0 else high if row > 7 else None
        across = []
        along = []
        for n in range(2):
            here = wind(n, row)
            across.append(roll(here, -1) - roll(here, 1))
            along.append(wind(n, row + 1) - wind(n, row - 1))
        scale = jnp.full((8, 128), 0.5, F32)
        if side is not None:
            scale = scale * side
        if mask is not None:
            scale = scale * mask
        field[0, row] = scale * (along[0] - across[1])
        field[1, row] = -scale * (across[0] + along[1])
    for step in range(STEPS):
        more = STEPS - 1 - step
        new = {}
        before = {}
        for row in range(-more - 1, 8 + more):
            xx, xy, yy = (kappa(q, row) for q in range(3))
            for n in range(2):
                here = field[n, row]
                gx = roll(here, -1) - here
                gy = field[n, row + 1] - here
                hx = xx * gx + xy * gy
                hy = xy * gx + yy * gy
                if row >= -more:
                    value = here - (roll(hx, 1) - hx + (before[n] - hy))
                    if row > 7:
                        value = value * high
                    if mask is not None:
                        value = value * mask
                    new[n, row] = value
                before[n] = hy
        field = new
    return field


def ends(pos, size):
    low = jnp.where(pos[0] == 0, 0.0, 1.0).astype(F32)
    high = jnp.where(pos[0] == size - 1, 0.0, 1.0).astype(F32)
    return low, high


def middle(size, pos, u, v, hu, hv, kt, kh, main):
    low, high = ends(pos, size)
    wind_refs = ((u, hu), (v, hv))

    def body(tile, _):
        field = diffuse(
            lambda n, row: wind_at(*wind_refs[n], row, tile),
            lambda q, row: kappa_at(kt, kh, q, row, tile),
            low,
            high,
            None,
        )
        for n in range(2):
            for y in range(8):
                start = pl.multiple_of(((n * 8 + y) * NT + tile) * 8, 8)
                main[pl.ds(start, 8), :] = field[n, y]
        return 0

    lax.fori_loop(0, NT, body, 0)


def finish(
    rows, columns, pos, rec_c, rec_d, sw, sk, main, norm, out, mw, mk, masks, sf
):
    low, high = ends(pos, rows)
    odd_col = (pos[1] & 1) == 1
    lane = lanes()
    fifth = lane % 16
    first = sublanes() == 0
    take_left = (fifth >= 1) & (fifth <= 5)
    take_right = (fifth >= 6) & (fifth <= 10)
    for k in range(NQ):
        i, t = k // 3, k % 3
        a = rec_c[i * 8 : i * 8 + 8, :]
        b = rec_d[i * 8 : i * 8 + 8, :]
        from_left = roll(jnp.where(odd_col, a, b), -5 * t)
        from_right = roll(jnp.where(odd_col, b, a), 5 - 5 * t)
        row = NM * 8 + k
        a = jnp.broadcast_to(rec_c[row : row + 1, :], (8, 128))
        b = jnp.broadcast_to(rec_d[row : row + 1, :], (8, 128))
        last = jnp.where(first == odd_col, a, b)
        src, dst, index = (sw, mw, k) if k < 36 else (sk, mk, k - 36)
        start = index * 24
        dst[start : start + 8, :] = jnp.where(take_left, from_left, src[start : start + 8, :])
        dst[start + 8 : start + 16, :] = jnp.where(
            take_right, from_right, src[start + 8 : start + 16, :]
        )
        take = (take_left & first) | (take_right & jnp.logical_not(first))
        dst[start + 16 : start + 24, :] = jnp.where(take, last, src[start + 16 : start + 24, :])
    west = jnp.where(pos[1] == 0, 0.0, 1.0).astype(F32)
    east = jnp.where(pos[1] == columns - 1, 0.0, 1.0).astype(F32)
    left_mask = jnp.where(fifth < 6, west, 1.0)
    right_mask = jnp.where((fifth >= 6) & (fifth < 12), east, 1.0)
    masks[0:8, :] = left_mask
    masks[8:16, :] = right_mask
    masks[16:24, :] = jnp.where(first, left_mask, right_mask)

    def body(tile, _):
        field = diffuse(
            lambda n, row: at(mw, (n * 18 + row + 5) * 3 + tile),
            lambda q, row: at(mk, (q * 15 + row + 4) * 3 + tile),
            low,
            high,
            at(masks, tile),
        )
        for n in range(2):
            for y in range(8):
                start = pl.multiple_of(((n * 8 + y) * 3 + tile) * 8, 8)
                sf[pl.ds(start, 8), :] = field[n, y]
        return 0

    lax.fori_loop(0, 3, body, 0)
    edge = (lane < 5) | (lane >= 123)
    for n in range(2):
        for y in range(8):
            start = (n * 8 + y) * 24
            both = jnp.where(take_left, sf[start + 8 : start + 16, :], sf[start : start + 8, :])
            for tile in range(8):
                place = ((n * 8 + y) * NT + tile) * 8
                value = jnp.where(edge, roll(both, -(16 * tile + 6)), main[place : place + 8, :])
                spot = pl.ds(n * 520 + tile * 64 + y, 8, stride=8)
                out[spot, :] = norm[spot, :] * value
            both = jnp.where(
                take_left,
                jnp.broadcast_to(sf[start + 17 : start + 18, :], (8, 128)),
                jnp.broadcast_to(sf[start + 16 : start + 17, :], (8, 128)),
            )
            place = ((n * 8 + y) * NT + 8) * 8
            value = jnp.where(edge, roll(both, -6), main[place : place + 8, :])
            spot = n * 520 + 512 + y
            out[spot : spot + 1, :] = norm[spot : spot + 1, :] * value[0:1, :]


def call(body, shapes, specs, scratch=(), cost=None):
    return pl.pallas_call(
        body,
        out_shape=[jax.ShapeDtypeStruct((n, 128), F32) for n in shapes],
        in_specs=specs,
        out_specs=[VM] * len(shapes),
        scratch_shapes=list(scratch),
        cost_estimate=cost,
        compiler_params=pltpu.CompilerParams(vmem_limit_bytes=32 << 20),
    )


def estimate(flops, bytes_accessed):
    return pl.CostEstimate(flops=flops, bytes_accessed=bytes_accessed, transcendentals=0)


def on_device(
    obs_resid, obs_cell, azimuth, gate_count, kappa_xx, kappa_yy, kappa_shear, norm_scale
):
    rows, columns = lax.axis_size("row"), lax.axis_size("col")
    pos = jnp.stack([lax.axis_index("row"), lax.axis_index("col")]).astype(jnp.int32)
    flat = lambda a: a.reshape(-1, 128)
    kt_rows = 3 * 8 * LV
    pay_rows = 96 + 4 * 3 * LV
    msg_rows = NM * 8 + 88
    pay_a, pay_b, kt = call(
        prepare, (pay_rows, pay_rows, kt_rows), [SM, SM] + [VM] * 6
    )(
        pos,
        gate_count,
        flat(obs_resid),
        flat(obs_cell),
        flat(azimuth),
        flat(kappa_xx),
        flat(kappa_yy),
        flat(kappa_shear),
    )
    rec_b = lax.ppermute(pay_b, "row", pairs(rows, 1))
    rec_a = lax.ppermute(pay_a, "row", pairs(rows, 0))
    work = (
        pltpu.VMEM((8 * LV, KC), BF16),
        pltpu.VMEM((256 * SPLITS, KC), BF16),
        pltpu.VMEM((64 + 64 * SPLITS, 128), F32),
    )
    u, v = call(
        own_wind, (8 * LV, 8 * LV), [VM], work, estimate(3_000_000_000, 2_000_000)
    )(pay_a[0:96])
    hu, hv, kh, sw, sk, msg_c, msg_d = call(
        edges,
        (10 * LV, 10 * LV, 7 * 3 * LV, 36 * 24, 45 * 24, msg_rows, msg_rows),
        [SM] + [VM] * 5,
        work,
    )(pos, rec_a, rec_b, u, v, kt)
    rec_c = lax.ppermute(msg_c, "col", pairs(columns, 0))
    rec_d = lax.ppermute(msg_d, "col", pairs(columns, 1))
    (main,) = call(
        lambda *refs: middle(rows, *refs),
        (16 * LV,),
        [SM] + [VM] * 6,
        (),
        estimate(3_000_000_000, 4_000_000),
    )(pos, u, v, hu, hv, kt, kh)
    (out,) = call(
        lambda *refs: finish(rows, columns, *refs),
        (2 * 65 * 8,),
        [SM] + [VM] * 6,
        (
            pltpu.VMEM((36 * 24, 128), F32),
            pltpu.VMEM((45 * 24, 128), F32),
            pltpu.VMEM((24, 128), F32),
            pltpu.VMEM((16 * 24, 128), F32),
        ),
    )(pos, rec_c, rec_d, sw, sk, main, flat(norm_scale))
    return out.reshape(norm_scale.shape)


def solution(mesh):
    in_specs = (
        P("row", "col"),
        P("row", "col"),
        P("row", "col"),
        P("row", "col"),
        P(None, "row", "col"),
        P(None, "row", "col"),
        P(None, "row", "col"),
        P(None, None, "row", "col"),
    )
    out_specs = P(None, None, "row", "col")
    return jax.shard_map(
        on_device, mesh=mesh, in_specs=in_specs, out_specs=out_specs, check_vma=False
    )
```

time: 211 us -> 56.4 us (0.27)
  the two profiles are of different devices: /device:TPU:62 before, /device:TPU:30 now
where the time goes in v1:
time: 56.4 us; the launch traced here: 55.9 us
  Pallas kernels  26.5 us (47%)
  starting transfers between devices  23.5 us (42%)
  local copies, waits for them, and re-layouts  4.3 us (8%)
  between operations  0.77 us (1%)
  waiting for transfers between devices  0.75 us (1%)
    ppermute x1, starting transfers between devices, on_device(): rec_b = lax.ppermute(pay_b, 'row', pairs(rows, 1))  14.3 us
    pallas_call x1, Pallas kernels, on_device(): call(edges, (10 * LV, 10 * LV, 7 * 3 * LV, 36 * 24, 45 * 24, msg_rows, ms...  11.6 us
    pallas_call x1, Pallas kernels, on_device(): call(lambda *refs: middle(rows, *refs), (16 * LV,), [SM] + [VM] * 6, (),...  6.57 us
    ppermute x1, starting transfers between devices, on_device(): rec_d = lax.ppermute(msg_d, 'col', pairs(columns, 1))  4.93 us
    unnamed x14, local copies, waits for them, and re-layouts  4.3 us
    pallas_call x1, Pallas kernels, on_device(): call(own_wind, (8 * LV, 8 * LV), [VM], work, estimate(3000000000, 2000000))  3.81 us
    pallas_call x1, Pallas kernels, on_device(): call(lambda *refs: finish(rows, columns, *refs), (2 * 65 * 8,), [SM] + [V...  3.8 us
    ppermute x1, starting transfers between devices, on_device(): rec_c = lax.ppermute(msg_c, 'col', pairs(columns, 0))  2.36 us
  transfers between devices with their start and end apart: 4, of which 1 were waited for; matrix products, arithmetic and copies ran while one was open for 0% of the time, Pallas kernels for 19%

profile of v1, /device:TPU:30, one launch (start us, length us, event | category | flops | bytes accessed | tf_op | source)
XLA Modules:
  0.0 55.9 jit_solution(10548124167703574454)
XLA Ops:
  0.0 0.0 copy-start.4
  0.7 0.1 pad_add_fusion.pos.refs_0_
  0.7 0.0 copy-done.4
  0.7 0.0 copy-start.1
  0.7 1.0 %copy-done.1 = f32[65,8,128]{2,1,0:T(8,128)S(1)} copy-done((f32[65,8,128]{2,1,0:T(8,128)S(1)}, f32[65,8,128]{2,1,0:T(8,128)}, u32[]{:S(2)}) %copy-start.1) | copy-done | bytes 266264
  1.7 0.0 copy-start.2
  1.7 0.9 %copy-done.2 = f32[65,8,128]{2,1,0:T(8,128)S(1)} copy-done((f32[65,8,128]{2,1,0:T(8,128)S(1)}, f32[65,8,128]{2,1,0:T(8,128)}, u32[]{:S(2)}) %copy-start.2) | copy-done | bytes 266264
  2.6 0.0 copy-start.3
  2.6 0.9 %copy-done.3 = f32[65,8,128]{2,1,0:T(8,128)S(1)} copy-done((f32[65,8,128]{2,1,0:T(8,128)S(1)}, f32[65,8,128]{2,1,0:T(8,128)}, u32[]{:S(2)}) %copy-start.3) | copy-done | bytes 266264
  3.6 0.0 copy-start.5
  3.6 0.7 %copy-done.5 = s32[1,4096]{1,0:T(1,128)S(1)} copy-done((s32[1,4096]{1,0:T(1,128)S(1)}, s32[1,4096]{1,0:T(1,128)}, u32[]{:S(2)}) %copy-start.5) | copy-done | bytes 16408
  4.3 0.0 copy-start.6
  4.3 0.7 %copy-done.6 = f32[1,4096]{1,0:T(1,128)S(1)} copy-done((f32[1,4096]{1,0:T(1,128)S(1)}, f32[1,4096]{1,0:T(1,128)}, u32[]{:S(2)}) %copy-start.6) | copy-done | bytes 16408
  5.0 0.8 %shard_map.82 = (f32[960,128]{1,0:T(8,128)S(1)}, f32[960,128]{1,0:T(8,128)S(1)}, f32[1728,128]{1,0:T(8,128)S(1)}) custom-call(s32[2]{0:T(128)S(1)} %pad_add_fusion.pos.refs_0_, s32[1,1]{1,0:T(1,128)S(6)} %copy.9.gate, f32[32,128]{1,0:T(8,128)S(1)} %bitcast.14, s32[32,128]{1,0:T(8,128)S(1)} %bitcast.15, f32[32,128]{1,0:T(8,128)S(1)} %bitcast.16, ...), custom_call_target="tpu_custom_call" | custom-call | tf_op jit(solution)/shard_map/pallas_call | solution.py:378
  5.8 14.3 %collective-permute-start.1 = (f32[960,128]{1,0:T(8,128)S(1)}, f32[960,128]{1,0:T(8,128)S(1)}, u32[]{:S(2)}, u32[]{:S(2)}) collective-permute-start(f32[960,128]{1,0:T(8,128)S(1)} %get-tuple-element.18), channel_id=1, source_target_pairs={{8,16},{16,8},{24,32},{32,24},{40,48},{48,40},{56,64},{64,56},{72,... | collective-permute-start | bytes 1474568 | tf_op jit(solution)/shard_map/ppermute | solution.py:390
  20.1 1.9 %collective-permute-start = (f32[960,128]{1,0:T(8,128)S(1)}, f32[960,128]{1,0:T(8,128)S(1)}, u32[]{:S(2)}, u32[]{:S(2)}) collective-permute-start(f32[960,128]{1,0:T(8,128)S(1)} %get-tuple-element.17), channel_id=1, source_target_pairs={{0,8},{8,0},{16,24},{24,16},{32,40},{40,32},{48,56},{56,48},{64,72... | collective-permute-start | bytes 1474568 | tf_op jit(solution)/shard_map/ppermute | solution.py:391
  22.1 3.8 %shard_map.83 = (f32[576,128]{1,0:T(8,128)S(1)}, f32[576,128]{1,0:T(8,128)S(1)}) custom-call(f32[96,128]{1,0:T(8,128)S(1)} %slice.3.obs), custom_call_target="tpu_custom_call" | custom-call | flops 3000000000 | bytes 2000000 | tf_op jit(solution)/shard_map/pallas_call | solution.py:397
  25.9 0.7 %collective-permute-done.1.rec_b = f32[960,128]{1,0:T(8,128)S(1)} collective-permute-done((f32[960,128]{1,0:T(8,128)S(1)}, f32[960,128]{1,0:T(8,128)S(1)}, u32[]{:S(2)}, u32[]{:S(2)}) %collective-permute-start.1) | collective-permute-done | bytes 491552 | tf_op jit(solution)/shard_map/ppermute | solution.py:390
  26.6 0.0 collective-permute-done.rec_a
  26.6 11.6 %shard_map.84 = (f32[720,128]{1,0:T(8,128)S(1)}, f32[720,128]{1,0:T(8,128)S(1)}, f32[1512,128]{1,0:T(8,128)S(1)}, f32[864,128]{1,0:T(8,128)S(1)}, f32[1080,128]{...) custom-call(s32[2]{0:T(128)S(1)} %pad_add_fusion.pos.refs_0_, ...), custom_call_target="tpu_custom_call" | custom-call | tf_op jit(solution)/shard_map/pallas_call | solution.py:400
  38.2 2.4 %collective-permute-start.2 = (f32[304,128]{1,0:T(8,128)S(1)}, f32[304,128]{1,0:T(8,128)S(1)}, u32[]{:S(2)}, u32[]{:S(2)}) collective-permute-start(f32[304,128]{1,0:T(8,128)S(1)} %get-tuple-element.22), channel_id=1, source_target_pairs={{0,1},{1,0},{2,3},{3,2},{4,5},{5,4},{6,7},{7,6},{8,9},{9,8},{10,11... | collective-permute-start | bytes 466952 | tf_op jit(solution)/shard_map/ppermute | solution.py:406
  40.5 4.9 %collective-permute-start.3 = (f32[304,128]{1,0:T(8,128)S(1)}, f32[304,128]{1,0:T(8,128)S(1)}, u32[]{:S(2)}, u32[]{:S(2)}) collective-permute-start(f32[304,128]{1,0:T(8,128)S(1)} %get-tuple-element.23), channel_id=1, source_target_pairs={{1,2},{2,1},{3,4},{4,3},{5,6},{6,5},{9,10},{10,9},{11,12},{12,11},... | collective-permute-start | bytes 466952 | tf_op jit(solution)/shard_map/ppermute | solution.py:407
  45.5 0.0 copy-start
  45.5 6.6 %shard_map.85.refs_5_ = f32[1152,128]{1,0:T(8,128)S(1)} custom-call(s32[2]{0:T(128)S(1)} %pad_add_fusion.pos.refs_0_, f32[576,128]{1,0:T(8,128)S(1)} %get-tuple-element.19.u.refs_1_, f32[576,128]{1,0:T(8,128)S(1)} %get-tuple-element.20.v.refs_2_, f32[720,128]{1,0:T(8,128)S(1)} %get-tuple-element.26.refs_3_, f32[720,128]{1,0:T(8,128)S(1)} %get-tuple-element.27.refs_4_, ...), custom_call_target="tpu_custom_call" | custom-call | flops 3000000000 | bytes 4000000 | tf_op jit(solution)/shard_map/pallas_call | solution.py:408
  52.1 0.0 collective-permute-done.2.refs_1_
  52.1 0.0 collective-permute-done.3.refs_2_
  52.1 0.0 copy-done
  52.1 3.8 %shard_map.86 = f32[1040,128]{1,0:T(8,128)} custom-call(s32[2]{0:T(128)S(1)} %pad_add_fusion.pos.refs_0_, f32[304,128]{1,0:T(8,128)S(1)} %collective-permute-done.2.refs_1_, f32[304,128]{1,0:T(8,128)S(1)} %collective-permute-done.3.refs_2_, f32[864,128]{1,0:T(8,128)S(1)} %get-tuple-element.24.refs_3_, f32[1080,128]{1,0:T(8,128)S(1)} %get-tuple-element.25.refs_4_, ...), custom_call_target="tpu_custom_call" | custom-call | tf_op jit(solution)/shard_map/pallas_call | solution.py:415
  (1 shorter events, 0.0 us)
Async XLA Ops:
  0.0 0.7 %copy-start.4 = (f32[1,4096]{1,0:T(1,128)S(1)}, f32[1,4096]{1,0:T(1,128)}, u32[]{:S(2)}) copy-start(f32[1,4096]{1,0:T(1,128)} %param.8) | copy-start | bytes 49156
  0.7 1.0 %copy-start.1 = (f32[65,8,128]{2,1,0:T(8,128)S(1)}, f32[65,8,128]{2,1,0:T(8,128)}, u32[]{:S(2)}) copy-start(f32[65,8,128]{2,1,0:T(8,128)} %param.12) | copy-start | bytes 798724
  1.7 1.0 %copy-start.2 = (f32[65,8,128]{2,1,0:T(8,128)S(1)}, f32[65,8,128]{2,1,0:T(8,128)}, u32[]{:S(2)}) copy-start(f32[65,8,128]{2,1,0:T(8,128)} %param.13) | copy-start | bytes 798724
  2.6 1.0 %copy-start.3 = (f32[65,8,128]{2,1,0:T(8,128)S(1)}, f32[65,8,128]{2,1,0:T(8,128)}, u32[]{:S(2)}) copy-start(f32[65,8,128]{2,1,0:T(8,128)} %param.14) | copy-start | bytes 798724
  3.6 0.7 %copy-start.5 = (s32[1,4096]{1,0:T(1,128)S(1)}, s32[1,4096]{1,0:T(1,128)}, u32[]{:S(2)}) copy-start(s32[1,4096]{1,0:T(1,128)} %param.9) | copy-start | bytes 49156
  4.3 0.7 %copy-start.6 = (f32[1,4096]{1,0:T(1,128)S(1)}, f32[1,4096]{1,0:T(1,128)}, u32[]{:S(2)}) copy-start(f32[1,4096]{1,0:T(1,128)} %param.10) | copy-start | bytes 49156
  5.8 20.8 %collective-permute-start.1 = (f32[960,128]{1,0:T(8,128)S(1)}, f32[960,128]{1,0:T(8,128)S(1)}, u32[]{:S(2)}, u32[]{:S(2)}) collective-permute-start(f32[960,128]{1,0:T(8,128)S(1)} %get-tuple-element.18), channel_id=1, source_target_pairs={{8,16},{16,8},{24,32},{32,24},{40,48},{48,40},{56,64},{64,56},{72,... | collective-permute-start | bytes 1474568 | tf_op jit(solution)/shard_map/ppermute | solution.py:390
  20.1 6.5 %collective-permute-start = (f32[960,128]{1,0:T(8,128)S(1)}, f32[960,128]{1,0:T(8,128)S(1)}, u32[]{:S(2)}, u32[]{:S(2)}) collective-permute-start(f32[960,128]{1,0:T(8,128)S(1)} %get-tuple-element.17), channel_id=1, source_target_pairs={{0,8},{8,0},{16,24},{24,16},{32,40},{40,32},{48,56},{56,48},{64,72... | collective-permute-start | bytes 1474568 | tf_op jit(solution)/shard_map/ppermute | solution.py:391
  38.2 13.9 %collective-permute-start.2 = (f32[304,128]{1,0:T(8,128)S(1)}, f32[304,128]{1,0:T(8,128)S(1)}, u32[]{:S(2)}, u32[]{:S(2)}) collective-permute-start(f32[304,128]{1,0:T(8,128)S(1)} %get-tuple-element.22), channel_id=1, source_target_pairs={{0,1},{1,0},{2,3},{3,2},{4,5},{5,4},{6,7},{7,6},{8,9},{9,8},{10,11... | collective-permute-start | bytes 466952 | tf_op jit(solution)/shard_map/ppermute | solution.py:406
  40.5 11.5 %collective-permute-start.3 = (f32[304,128]{1,0:T(8,128)S(1)}, f32[304,128]{1,0:T(8,128)S(1)}, u32[]{:S(2)}, u32[]{:S(2)}) collective-permute-start(f32[304,128]{1,0:T(8,128)S(1)} %get-tuple-element.23), channel_id=1, source_target_pairs={{1,2},{2,1},{3,4},{4,3},{5,6},{6,5},{9,10},{10,9},{11,12},{12,11},... | collective-permute-start | bytes 466952 | tf_op jit(solution)/shard_map/ppermute | solution.py:407
  45.5 6.6 %copy-start = (f32[2,65,8,128]{3,2,1,0:T(8,128)S(1)}, f32[2,65,8,128]{3,2,1,0:T(8,128)}, u32[]{:S(2)}) copy-start(f32[2,65,8,128]{3,2,1,0:T(8,128)} %param.15) | copy-start | bytes 1597444

commit v2 on v0

v2 whole, which is shorter than its diff:
```python
import jax
import jax.numpy as jnp
from jax import lax
from jax.experimental import pallas as pl
from jax.experimental.pallas import tpu as pltpu
from jax.sharding import PartitionSpec as P

STEPS = 4
NT = 8
F32 = jnp.float32
BF16 = jnp.bfloat16
KC = 1024
SPLITS = 2
NQ = 81
NM = NQ // 3
GROUP = 2
PAY = 96 + 12 * 64 + 16
TAB = 320 + 64 * SPLITS
OWN = 8 * 64 + 16
HALO = 5 * 64 + 16
HB = pl.BlockSpec(memory_space=pltpu.HBM)
VM = pl.BlockSpec(memory_space=pltpu.VMEM)
SM = pl.BlockSpec(memory_space=pltpu.SMEM)


def pairs(size, first):
    out = []
    for i in range(first, size - 1, 2):
        out += [(i, i + 1), (i + 1, i)]
    return out


def roll(x, by):
    by = by % 128
    return x if by == 0 else pltpu.roll(x, by, 1)


def at(ref, i):
    return ref[pl.ds(pl.multiple_of(i * 8, 8), 8), :]


def wide(ref, row):
    return jnp.broadcast_to(ref[row : row + 1, :], (8, 128))


def lanes():
    return lax.broadcasted_iota(jnp.int32, (8, 128), 1)


def sublanes():
    return lax.broadcasted_iota(jnp.int32, (8, 128), 0)


def prepare(pos, gate, resid_h, cell_h, azimuth_h, kxx_h, kyy_h, ksh_h, pay_a, pay_b, kt,
            resid, cell, azimuth, kxx, kyy, ksh, sems):
    copies = []
    for i, (src, dst) in enumerate(
        (
            (resid_h, resid),
            (cell_h, cell),
            (azimuth_h, azimuth),
            (kxx_h, kxx),
            (kyy_h, kyy),
            (ksh_h, ksh),
        )
    ):
        copies.append(pltpu.make_async_copy(src, dst, sems.at[i]))
        copies[-1].start()
    odd = (pos[0] & 1) == 1
    slot = lax.broadcasted_iota(jnp.int32, (32, 128), 0) * 128 + lax.broadcasted_iota(
        jnp.int32, (32, 128), 1
    )
    for copy in copies[:3]:
        copy.wait()
    weight = jnp.where(slot < gate[0, 0], resid[...], 0.0)
    angle = azimuth[...]
    wu = weight * jnp.sin(angle)
    wv = weight * jnp.cos(angle)
    cf = cell[...].astype(F32)
    for pay in (pay_a, pay_b):
        pay[0:32, :] = wu
        pay[32:64, :] = wv
        pay[64:96, :] = cf
        pay[876:880, :] = jnp.zeros((4, 128), F32)
    for copy in copies[3:]:
        copy.wait()

    def entries(get):
        xx, yy = get(kxx), get(kyy)
        return xx, get(ksh) * jnp.sqrt(xx * yy), yy

    for tile in range(NT):
        rows = []
        for y in range(8):
            rows.append(entries(lambda ref: ref[pl.ds(tile * 64 + y, 8, stride=8), :]))
            for q in range(3):
                start = (q * 8 + y) * 64 + tile * 8
                kt[start : start + 8, :] = rows[y][q]
        for i in range(4):
            for q in range(3):
                start = 96 + (i * 3 + q) * 64 + tile * 8
                low, high = rows[i][q], rows[i + 4][q]
                pay_a[start : start + 8, :] = jnp.where(odd, low, high)
                pay_b[start : start + 8, :] = jnp.where(odd, high, low)
    last = entries(lambda ref: ref[512:520, :])
    for q in range(3):
        kt[1536 + q * 8 : 1544 + q * 8, :] = last[q]
        for i in range(4):
            start = 864 + i * 3 + q
            low, high = last[q][i : i + 1, :], last[q][i + 4 : i + 5, :]
            pay_a[start : start + 1, :] = jnp.where(odd, low, high)
            pay_b[start : start + 1, :] = jnp.where(odd, high, low)


def scatter(jobs, hots, vals, tab, out_u, out_v):
    first = lax.broadcasted_iota(jnp.int32, (16, 128), 0).astype(F32)
    iota = [(first + 16.0 * b).astype(BF16) for b in range(8)]
    one = jnp.full((16, 128), 1, BF16)
    zero = jnp.full((16, 128), 0, BF16)
    per = KC // 128
    chunks = 4096 // KC
    for job, (wu, wv, cf, shift, ny, _) in enumerate(jobs):
        cell = cf.astype(jnp.int32)
        level = lax.shift_right_logical(cell, 10)
        row = (lax.shift_right_logical(cell, 7) & 7) - shift
        lf = level.astype(F32)
        index = [jnp.where((row == y) & (level < 64), lf, -1.0) for y in range(ny)]
        index += [jnp.full((32, 128), -1.0, F32)] * (8 - ny)
        index.append(jnp.where((level == 64) & (row < ny), row.astype(F32), -1.0))
        index.append((cell & 127).astype(F32))
        for value in (wu, wv):
            for s in range(SPLITS):
                top = value.astype(BF16).astype(F32)
                value = value - top
                index.append(top)
        for k, value in enumerate(index):
            start = job * TAB + k * 32
            tab[start : start + 32, :] = value

    def build(job, c):
        ny = jobs[job][4]
        for j in range(per):

            def spread(k):
                i = job * TAB + k * 32 + c * per + j
                return jnp.broadcast_to(tab[i : i + 1, :], (16, 128)).astype(BF16)

            rows = []
            for y in range(ny):
                index = spread(y)
                for b in range(4):
                    rows.append(jnp.where(iota[b] == index, one, zero))
            rows.append(jnp.where(iota[0] == spread(8), one, zero))
            hot[job, c, j] = jnp.concatenate(rows, axis=0)
            col = spread(9)
            parts = [spread(10 + k) for k in range(2 * SPLITS)]
            hits = [iota[b] == col for b in range(8)]
            val[job, c, j] = jnp.concatenate(
                [
                    jnp.where(hit, parts[n * SPLITS + s], zero)
                    for s in range(SPLITS)
                    for n in range(2)
                    for hit in hits
                ],
                axis=0,
            )

    def multiply(job, c):
        ny, base = jobs[job][4:]
        count = ny * 64 + 16
        total = None
        left = jnp.concatenate([hot[job, c, j] for j in range(per)], axis=1)
        for s in range(SPLITS):
            part = lax.dot_general(
                left,
                jnp.concatenate(
                    [val[job, c, j][s * 256 : s * 256 + 256] for j in range(per)], axis=1
                ),
                (((1,), (1,)), ((), ())),
                preferred_element_type=F32,
            )
            total = part if total is None else total + part
        for ref, part in ((out_u, total[:, 0:128]), (out_v, total[:, 128:256])):
            if c > 0:
                part = part + ref[base : base + count, :]
            ref[base : base + count, :] = part

    hot, val = {}, {}
    steps = [(job, c) for job in range(len(jobs)) for c in range(chunks)]
    build(*steps[0])
    for now, later in zip(steps, steps[1:] + [None]):
        if later is not None:
            build(*later)
        multiply(*now)


def wind_at(own, halo, row, tile):
    if 0 <= row < 8:
        return wide(own, 512 + row) if tile is None else at(own, row * NT + tile)
    base, row = (0, row + 5) if row < 0 else (HALO, row - 8)
    if tile is None:
        return wide(halo, base + 320 + row)
    return at(halo, base // 8 + row * NT + tile)


def kappa_at(kt, halo, q, row, tile):
    if 0 <= row < 8:
        row = q * 8 + row
        return wide(kt, 1536 + row) if tile is None else at(kt, row * NT + tile)
    row = ((row + 4) if row < 0 else row - 4) * 3 + q
    return wide(halo, 1344 + row) if tile is None else at(halo, row * NT + tile)


def strip(get, ref, index):
    lane = lanes()
    left_slot = lane // 16
    right_slot = ((lane + 4) % 128) // 16
    left = right = None
    for j in range(8):
        moved = roll(get(j), 16 * j + 6)
        left = moved if j == 0 else jnp.where(left_slot == j, moved, left)
        right = moved if j == 0 else jnp.where(right_slot == j, moved, right)
    whole = get(None)
    last = jnp.where(sublanes() == 2, whole, roll(whole, 6))
    start = index * 24
    ref[start : start + 8, :] = left
    ref[start + 8 : start + 16, :] = right
    ref[start + 16 : start + 24, :] = last


def own_part(obs, kt, u, v, sw, sk, hot_a, hot_b, val_a, val_b, tab):
    job = (obs[0:32, :], obs[32:64, :], obs[64:96, :], 0, 8, 0)
    scatter([job], (hot_a, hot_b), (val_a, val_b), tab, u, v)
    for y in range(8):
        for n, ref in enumerate((u, v)):
            strip(lambda t: wind_at(ref, None, y, t), sw, n * 8 + y)
        for q in range(3):
            strip(lambda t: kappa_at(kt, None, q, y, t), sk, q * 8 + y)


def strip_place(k, sw, sk, tw, tk):
    if k < 36:
        n, row = k // 18, k % 18 - 5
        if 0 <= row < 8:
            return sw, n * 8 + row
        return tw, n * 10 + ((row + 5) if row < 0 else row - 3)
    q, row = (k - 36) // 15, (k - 36) % 15 - 4
    if 0 <= row < 8:
        return sk, q * 8 + row
    return tk, q * 7 + ((row + 4) if row < 0 else row - 4)


def edges(pos, rec_a, rec_b, sw, sk, hu, hv, kh, tw, tk, msg_c, msg_d,
          hot_a, hot_b, val_a, val_b, tab):
    odd = (pos[0] & 1) == 1
    for q in range(3):
        for j in range(7):
            row, one, two = (j, rec_a, rec_b) if j < 4 else (j - 4, rec_b, rec_a)
            src = 96 + (row * 3 + q) * 64
            dst = (j * 3 + q) * 64
            kh[dst : dst + 64, :] = jnp.where(odd, one[src : src + 64, :], two[src : src + 64, :])
            src, dst = 864 + row * 3 + q, 1344 + j * 3 + q
            kh[dst : dst + 1, :] = jnp.where(odd, one[src : src + 1, :], two[src : src + 1, :])
    kh[1365:1368, :] = jnp.zeros((3, 128), F32)
    jobs = []
    for side in range(2):
        one, two = (rec_a, rec_b) if side == 0 else (rec_b, rec_a)
        part = jnp.where(odd, one[0:96, :], two[0:96, :])
        jobs.append((part[0:32], part[32:64], part[64:96], 3 - 3 * side, 5, side * HALO))
    scatter(jobs, (hot_a, hot_b), (val_a, val_b), tab, hu, hv)
    for i in range(10):
        row = i - 5 if i < 5 else i + 3
        for n, ref in enumerate((hu, hv)):
            strip(lambda t: wind_at(None, ref, row, t), tw, n * 10 + i)
    for i in range(7):
        row = i - 4 if i < 4 else i + 4
        for q in range(3):
            strip(lambda t: kappa_at(None, kh, q, row, t), tk, q * 7 + i)
    fifth = lanes() % 16
    odd_col = (pos[1] & 1) == 1
    for i in range(NM):
        packed = []
        for t in range(3):
            ref, index = strip_place(3 * i + t, sw, sk, tw, tk)
            left = ref[index * 24 : index * 24 + 8, :]
            packed.append((roll(left, 5 * t), roll(left, 5 * t - 5)))
            row = NM * 8 + 3 * i + t
            last = ref[index * 24 + 16 : index * 24 + 17, :]
            msg_c[row : row + 1, :] = last
            msg_d[row : row + 1, :] = last
        right_edge, left_edge = (
            jnp.where(fifth < 6, packed[0][e], jnp.where(fifth < 11, packed[1][e], packed[2][e]))
            for e in range(2)
        )
        msg_c[i * 8 : i * 8 + 8, :] = jnp.where(odd_col, left_edge, right_edge)
        msg_d[i * 8 : i * 8 + 8, :] = jnp.where(odd_col, right_edge, left_edge)
    fill = NM * 8 + NQ
    for msg in (msg_c, msg_d):
        msg[fill : fill + 7, :] = jnp.zeros((7, 128), F32)


def derive(wind, low, high, mask, put):
    for row in range(-4, 12):
        side = low if row < 0 else high if row > 7 else None
        across = []
        along = []
        for n in range(2):
            here = wind(n, row)
            across.append(roll(here, -1) - roll(here, 1))
            along.append(wind(n, row + 1) - wind(n, row - 1))
        scale = 0.5 if side is None else 0.5 * side
        if mask is not None:
            scale = scale * mask
        put(0, row, scale * (along[0] - across[1]))
        put(1, row, -scale * (across[0] + along[1]))


def advance(more, field, kappa, high, mask, put):
    before = {}
    here = [field(n, -more - 1) for n in range(2)]
    for row in range(-more - 1, 8 + more):
        xx, xy, yy = (kappa(q, row) for q in range(3))
        for n in range(2):
            below = field(n, row + 1)
            gx = roll(here[n], -1) - here[n]
            gy = below - here[n]
            hx = xx * gx + xy * gy
            hy = xy * gx + yy * gy
            if row >= -more:
                value = here[n] - (roll(hx, 1) - hx + (before[n] - hy))
                if row > 7:
                    value = value * high
                if mask is not None:
                    value = value * mask
                put(n, row, value)
            before[n] = hy
            here[n] = below


def slab(ref, tiles, tile):
    def get(n, row):
        return at(ref, (n * 16 + row + 4) * tiles + tile)

    def put(n, row, value):
        start = ((n * 16 + row + 4) * tiles + tile) * 8
        ref[pl.ds(pl.multiple_of(start, 8), 8), :] = value

    return get, put


def ends(pos, size):
    low = jnp.where(pos[0] == 0, 0.0, 1.0).astype(F32)
    high = jnp.where(pos[0] == size - 1, 0.0, 1.0).astype(F32)
    return low, high


def middle(size, pos, u, v, hu, hv, kt, kh, main, fa, fb):
    low, high = ends(pos, size)
    wind_refs = ((u, hu), (v, hv))

    def stage(step):
        def body(g, _):
            for k in range(GROUP):
                tile = g * GROUP + k
                if step < 0:
                    put = slab(fa, NT, tile)[1]
                    derive(lambda n, row: wind_at(*wind_refs[n], row, tile), low, high, None, put)
                    continue
                src, dst = (fa, fb) if step % 2 == 0 else (fb, fa)
                put = slab(dst, NT, tile)[1]
                if step == STEPS - 1:

                    def put(n, row, value):
                        start = pl.multiple_of(((n * 8 + row) * NT + tile) * 8, 8)
                        main[pl.ds(start, 8), :] = value

                advance(
                    STEPS - 1 - step,
                    slab(src, NT, tile)[0],
                    lambda q, row: kappa_at(kt, kh, q, row, tile),
                    high,
                    None,
                    put,
                )
            return 0

        lax.fori_loop(0, NT // GROUP, body, 0)

    for step in range(-1, STEPS):
        stage(step)


def finish(
    rows, columns, pos, rec_c, rec_d, sw, sk, tw, tk, main, norm, out, mw, mk, masks, fa, fb
):
    low, high = ends(pos, rows)
    odd_col = (pos[1] & 1) == 1
    lane = lanes()
    fifth = lane % 16
    sub = sublanes()
    take_left = (fifth >= 1) & (fifth <= 5)
    take_right = (fifth >= 6) & (fifth <= 10)
    take_last = (take_left & (sub == 0)) | (take_right & (sub == 1))
    for k in range(NQ):
        i, t = k // 3, k % 3
        a = rec_c[i * 8 : i * 8 + 8, :]
        b = rec_d[i * 8 : i * 8 + 8, :]
        from_left = roll(jnp.where(odd_col, a, b), -5 * t)
        from_right = roll(jnp.where(odd_col, b, a), 5 - 5 * t)
        row = NM * 8 + k
        last = jnp.where((sub == 0) == odd_col, wide(rec_c, row), wide(rec_d, row))
        src, index = strip_place(k, sw, sk, tw, tk)
        here = index * 24
        dst, start = (mw, k * 24) if k < 36 else (mk, (k - 36) * 24)
        dst[start : start + 8, :] = jnp.where(take_left, from_left, src[here : here + 8, :])
        dst[start + 8 : start + 16, :] = jnp.where(
            take_right, from_right, src[here + 8 : here + 16, :]
        )
        dst[start + 16 : start + 24, :] = jnp.where(take_last, last, src[here + 16 : here + 24, :])
    west = jnp.where(pos[1] == 0, 0.0, 1.0).astype(F32)
    east = jnp.where(pos[1] == columns - 1, 0.0, 1.0).astype(F32)
    left_mask = jnp.where(fifth < 6, west, 1.0)
    right_mask = jnp.where((fifth >= 6) & (fifth < 12), east, 1.0)
    masks[0:8, :] = left_mask
    masks[8:16, :] = right_mask
    masks[16:24, :] = jnp.where(sub == 0, left_mask, jnp.where(sub == 1, right_mask, 1.0))
    for step in range(-1, STEPS):
        for tile in range(3):
            mask = masks[tile * 8 : tile * 8 + 8, :]
            src, dst = (fa, fb) if step % 2 == 0 else (fb, fa)
            put = slab(dst, 3, tile)[1]
            if step < 0:
                derive(
                    lambda n, row: at(mw, (n * 18 + row + 5) * 3 + tile), low, high, mask, put
                )
            else:
                advance(
                    STEPS - 1 - step,
                    slab(src, 3, tile)[0],
                    lambda q, row: at(mk, (q * 15 + row + 4) * 3 + tile),
                    high,
                    mask,
                    put,
                )
    done = fb if STEPS % 2 == 1 else fa
    edge = (lane < 5) | (lane >= 123)
    for n in range(2):
        for y in range(8):
            left, right, last = (slab(done, 3, tile)[0](n, y) for tile in range(3))
            both = jnp.where(take_left, right, left)
            for tile in range(NT):
                place = ((n * 8 + y) * NT + tile) * 8
                value = jnp.where(edge, roll(both, -(16 * tile + 6)), main[place : place + 8, :])
                spot = pl.ds(n * 520 + tile * 64 + y, 8, stride=8)
                out[spot, :] = norm[spot, :] * value
            both = roll(jnp.where(take_left[0:1], last[1:2], last[0:1]), -6)
            value = jnp.where(edge[0:1], both, last[2:3])
            spot = n * 520 + 512 + y
            out[spot : spot + 1, :] = norm[spot : spot + 1, :] * value


def call(body, shapes, specs, scratch=(), cost=None):
    return pl.pallas_call(
        body,
        out_shape=[jax.ShapeDtypeStruct((n, 128), F32) for n in shapes],
        in_specs=specs,
        out_specs=[VM] * len(shapes),
        scratch_shapes=list(scratch),
        cost_estimate=cost,
        compiler_params=pltpu.CompilerParams(vmem_limit_bytes=32 << 20),
    )


def estimate(flops, bytes_accessed):
    return pl.CostEstimate(flops=flops, bytes_accessed=bytes_accessed, transcendentals=0)


def on_device(
    obs_resid, obs_cell, azimuth, gate_count, kappa_xx, kappa_yy, kappa_shear, norm_scale
):
    rows, columns = lax.axis_size("row"), lax.axis_size("col")
    pos = jnp.stack([lax.axis_index("row"), lax.axis_index("col")]).astype(jnp.int32)
    flat = lambda a: a.reshape(-1, 128)
    buffers = lambda *shapes: tuple(pltpu.VMEM((n, 128), t) for n, t in shapes)
    pay_a, pay_b, kt = call(
        prepare,
        (PAY, PAY, 24 * 64 + 24),
        [SM, SM] + [HB] * 6,
        buffers((32, F32), (32, jnp.int32), (32, F32), (520, F32), (520, F32), (520, F32))
        + (pltpu.SemaphoreType.DMA((6,)),),
    )(
        pos,
        gate_count,
        *(
            pltpu.with_memory_space_constraint(flat(a), pltpu.HBM)
            for a in (obs_resid, obs_cell, azimuth, kappa_xx, kappa_yy, kappa_shear)
        ),
    )
    rec_b = lax.ppermute(pay_b, "row", pairs(rows, 1))
    rec_a = lax.ppermute(pay_a, "row", pairs(rows, 0))
    work = (
        pltpu.VMEM((KC // 128, OWN, 128), BF16),
        pltpu.VMEM((KC // 128, OWN, 128), BF16),
        pltpu.VMEM((KC // 128, 256 * SPLITS, 128), BF16),
        pltpu.VMEM((KC // 128, 256 * SPLITS, 128), BF16),
        pltpu.VMEM((2 * TAB, 128), F32),
    )
    u, v, sw, sk = call(
        own_part,
        (OWN, OWN, 16 * 24, 24 * 24),
        [VM] * 2,
        work,
        estimate(3_000_000_000, 2_000_000),
    )(pay_a[0:96], kt)
    hu, hv, kh, tw, tk, msg_c, msg_d = call(
        edges,
        (2 * HALO, 2 * HALO, 21 * 64 + 24, 20 * 24, 21 * 24, NM * 8 + 88, NM * 8 + 88),
        [SM] + [VM] * 4,
        work,
    )(pos, rec_a, rec_b, sw, sk)
    rec_c = lax.ppermute(msg_c, "col", pairs(columns, 0))
    rec_d = lax.ppermute(msg_d, "col", pairs(columns, 1))
    (main,) = call(
        lambda *refs: middle(rows, *refs),
        (16 * 64,),
        [SM] + [VM] * 6,
        buffers((32 * 64, F32), (32 * 64, F32)),
        estimate(3_000_000_000, 4_000_000),
    )(pos, u, v, hu, hv, kt, kh)
    (out,) = call(
        lambda *refs: finish(rows, columns, *refs),
        (2 * 65 * 8,),
        [SM] + [VM] * 8,
        buffers((36 * 24, F32), (45 * 24, F32), (24, F32), (32 * 24, F32), (32 * 24, F32)),
    )(pos, rec_c, rec_d, sw, sk, tw, tk, main, flat(norm_scale))
    return out.reshape(norm_scale.shape)


def solution(mesh):
    in_specs = (
        P("row", "col"),
        P("row", "col"),
        P("row", "col"),
        P("row", "col"),
        P(None, "row", "col"),
        P(None, "row", "col"),
        P(None, "row", "col"),
        P(None, None, "row", "col"),
    )
    out_specs = P(None, None, "row", "col")
    return jax.shard_map(
        on_device, mesh=mesh, in_specs=in_specs, out_specs=out_specs, check_vma=False
    )
```

time: 211 us -> 42.1 us (0.20)
  the two profiles are of different devices: /device:TPU:62 before, /device:TPU:30 now
where the time goes in v2:
time: 42.1 us; the launch traced here: 41.8 us
  starting transfers between devices  23.5 us (56%)
  Pallas kernels  15.9 us (38%)
  waiting for transfers between devices  1.56 us (4%)
  between operations  0.75 us (2%)
    ppermute x1, starting transfers between devices, on_device(): rec_b = lax.ppermute(pay_b, 'row', pairs(rows, 1))  14.3 us
    ppermute x1, starting transfers between devices, on_device(): rec_d = lax.ppermute(msg_d, 'col', pairs(columns, 1))  4.93 us
    pallas_call x1, Pallas kernels, on_device(): call(lambda *refs: middle(rows, *refs), (16 * 64,), [SM] + [VM] * 6, buff...  4.85 us
    pallas_call x1, Pallas kernels, on_device(): call(edges, (2 * HALO, 2 * HALO, 21 * 64 + 24, 20 * 24, 21 * 24, NM * 8 +...  3.87 us
    pallas_call x1, Pallas kernels, on_device(): call(lambda *refs: finish(rows, columns, *refs), (2 * 65 * 8,), [SM] + [V...  2.66 us
    pallas_call x1, Pallas kernels, on_device(): call(own_part, (OWN, OWN, 16 * 24, 24 * 24), [VM] * 2, work, estimate(300...  2.56 us
    ppermute x1, starting transfers between devices, on_device(): rec_c = lax.ppermute(msg_c, 'col', pairs(columns, 0))  2.36 us
    pallas_call x1, Pallas kernels, on_device(): call(prepare, (PAY, PAY, 24 * 64 + 24), [SM, SM] + [HB] * 6, buffers((32,...  1.94 us
  transfers between devices with their start and end apart: 4, of which 1 were waited for; matrix products, arithmetic and copies ran while one was open for 0% of the time, Pallas kernels for 18%

profile of v2, /device:TPU:30, one launch (start us, length us, event | category | flops | bytes accessed | tf_op | source)
XLA Modules:
  0.0 41.8 jit_solution(8304614026179109899)
XLA Ops:
  0.7 0.1 pad_add_fusion.pos.refs_0_
  0.7 1.9 %shard_map.82 = (f32[880,128]{1,0:T(8,128)S(1)}, f32[880,128]{1,0:T(8,128)S(1)}, f32[1560,128]{1,0:T(8,128)S(1)}) custom-call(s32[2]{0:T(128)S(1)} %pad_add_fusion.pos.refs_0_, s32[1,1]{1,0:T(1,128)S(6)} %copy.9.gate, f32[32,128]{1,0:T(8,128)} %bitcast.14, s32[32,128]{1,0:T(8,128)} %bitcast.15, f32[32,128]{1,0:T(8,128)} %bitcast.16, f32[520,128]{1,0:T(8,128)} %bitcast.11, ...), custom_call_target="tpu_custom_call" | custom-call | tf_op jit(solution)/shard_map/pallas_call | solution.py:485
  2.7 14.3 %collective-permute-start.1 = (f32[880,128]{1,0:T(8,128)S(1)}, f32[880,128]{1,0:T(8,128)S(1)}, u32[]{:S(2)}, u32[]{:S(2)}) collective-permute-start(f32[880,128]{1,0:T(8,128)S(1)} %get-tuple-element.20), channel_id=1, source_target_pairs={{8,16},{16,8},{24,32},{32,24},{40,48},{48,40},{56,64},{64,56},{72,... | collective-permute-start | bytes 1351688 | tf_op jit(solution)/shard_map/ppermute | solution.py:499
  17.0 1.9 %collective-permute-start = (f32[880,128]{1,0:T(8,128)S(1)}, f32[880,128]{1,0:T(8,128)S(1)}, u32[]{:S(2)}, u32[]{:S(2)}) collective-permute-start(f32[880,128]{1,0:T(8,128)S(1)} %get-tuple-element.19), channel_id=1, source_target_pairs={{0,8},{8,0},{16,24},{24,16},{32,40},{40,32},{48,56},{56,48},{64,72... | collective-permute-start | bytes 1351688 | tf_op jit(solution)/shard_map/ppermute | solution.py:500
  18.9 2.6 %shard_map.83 = (f32[528,128]{1,0:T(8,128)S(1)}, f32[528,128]{1,0:T(8,128)S(1)}, f32[384,128]{1,0:T(8,128)S(1)}, f32[576,128]{1,0:T(8,128)S(1)}) custom-call(f32[96,128]{1,0:T(8,128)S(1)} %slice.3.obs, f32[1560,128]{1,0:T(8,128)S(1)} %get-tuple-element.21.kt.refs_5_), custom_call_target="tpu_custom_call" | custom-call | flops 3000000000 | bytes 2000000 | tf_op jit(solution)/shard_map/pallas_call | solution.py:508
  21.5 1.6 %collective-permute-done.1.rec_b = f32[880,128]{1,0:T(8,128)S(1)} collective-permute-done((f32[880,128]{1,0:T(8,128)S(1)}, f32[880,128]{1,0:T(8,128)S(1)}, u32[]{:S(2)}, u32[]{:S(2)}) %collective-permute-start.1) | collective-permute-done | bytes 450592 | tf_op jit(solution)/shard_map/ppermute | solution.py:499
  23.0 0.0 collective-permute-done.rec_a
  23.0 3.9 %shard_map.84 = (f32[672,128]{1,0:T(8,128)S(1)}, f32[672,128]{1,0:T(8,128)S(1)}, f32[1368,128]{1,0:T(8,128)S(1)}, f32[480,128]{1,0:T(8,128)S(1)}, f32[504,128]{1...) custom-call(s32[2]{0:T(128)S(1)} %pad_add_fusion.pos.refs_0_, ...), custom_call_target="tpu_custom_call" | custom-call | tf_op jit(solution)/shard_map/pallas_call | solution.py:515
  26.9 2.4 %collective-permute-start.2 = (f32[304,128]{1,0:T(8,128)S(1)}, f32[304,128]{1,0:T(8,128)S(1)}, u32[]{:S(2)}, u32[]{:S(2)}) collective-permute-start(f32[304,128]{1,0:T(8,128)S(1)} %get-tuple-element.24), channel_id=1, source_target_pairs={{0,1},{1,0},{2,3},{3,2},{4,5},{5,4},{6,7},{7,6},{8,9},{9,8},{10,11... | collective-permute-start | bytes 466952 | tf_op jit(solution)/shard_map/ppermute | solution.py:521
  29.3 4.9 %collective-permute-start.3 = (f32[304,128]{1,0:T(8,128)S(1)}, f32[304,128]{1,0:T(8,128)S(1)}, u32[]{:S(2)}, u32[]{:S(2)}) collective-permute-start(f32[304,128]{1,0:T(8,128)S(1)} %get-tuple-element.25), channel_id=1, source_target_pairs={{1,2},{2,1},{3,4},{4,3},{5,6},{6,5},{9,10},{10,9},{11,12},{12,11},... | collective-permute-start | bytes 466952 | tf_op jit(solution)/shard_map/ppermute | solution.py:522
  34.2 0.0 copy-start
  34.2 4.8 %shard_map.85.refs_7_ = f32[1024,128]{1,0:T(8,128)S(1)} custom-call(s32[2]{0:T(128)S(1)} %pad_add_fusion.pos.refs_0_, f32[528,128]{1,0:T(8,128)S(1)} %get-tuple-element.28.refs_1_, f32[528,128]{1,0:T(8,128)S(1)} %get-tuple-element.29.refs_2_, f32[672,128]{1,0:T(8,128)S(1)} %get-tuple-element.30.refs_3_, f32[672,128]{1,0:T(8,128)S(1)} %get-tuple-element.31.refs_4_, ...), custom_call_target="tpu_custom_call" | custom-call | flops 3000000000 | bytes 4000000 | tf_op jit(solution)/shard_map/pallas_call | solution.py:523
  39.1 0.0 collective-permute-done.2.refs_1_
  39.1 0.0 collective-permute-done.3.refs_2_
  39.1 0.0 copy-done
  39.1 2.7 %shard_map.86 = f32[1040,128]{1,0:T(8,128)} custom-call(s32[2]{0:T(128)S(1)} %pad_add_fusion.pos.refs_0_, f32[304,128]{1,0:T(8,128)S(1)} %collective-permute-done.2.refs_1_, f32[304,128]{1,0:T(8,128)S(1)} %collective-permute-done.3.refs_2_, f32[384,128]{1,0:T(8,128)S(1)} %get-tuple-element.22.sw.refs_3_, f32[576,128]{1,0:T(8,128)S(1)} %get-tuple-element.23.sk.refs_4_, ...), custom_call_target="tpu_custom_call" | custom-call | tf_op jit(solution)/shard_map/pallas_call | solution.py:530
  (1 shorter events, 0.0 us)
Async XLA Ops:
  2.7 20.4 %collective-permute-start.1 = (f32[880,128]{1,0:T(8,128)S(1)}, f32[880,128]{1,0:T(8,128)S(1)}, u32[]{:S(2)}, u32[]{:S(2)}) collective-permute-start(f32[880,128]{1,0:T(8,128)S(1)} %get-tuple-element.20), channel_id=1, source_target_pairs={{8,16},{16,8},{24,32},{32,24},{40,48},{48,40},{56,64},{64,56},{72,... | collective-permute-start | bytes 1351688 | tf_op jit(solution)/shard_map/ppermute | solution.py:499
  17.0 6.1 %collective-permute-start = (f32[880,128]{1,0:T(8,128)S(1)}, f32[880,128]{1,0:T(8,128)S(1)}, u32[]{:S(2)}, u32[]{:S(2)}) collective-permute-start(f32[880,128]{1,0:T(8,128)S(1)} %get-tuple-element.19), channel_id=1, source_target_pairs={{0,8},{8,0},{16,24},{24,16},{32,40},{40,32},{48,56},{56,48},{64,72... | collective-permute-start | bytes 1351688 | tf_op jit(solution)/shard_map/ppermute | solution.py:500
  26.9 12.2 %collective-permute-start.2 = (f32[304,128]{1,0:T(8,128)S(1)}, f32[304,128]{1,0:T(8,128)S(1)}, u32[]{:S(2)}, u32[]{:S(2)}) collective-permute-start(f32[304,128]{1,0:T(8,128)S(1)} %get-tuple-element.24), channel_id=1, source_target_pairs={{0,1},{1,0},{2,3},{3,2},{4,5},{5,4},{6,7},{7,6},{8,9},{9,8},{10,11... | collective-permute-start | bytes 466952 | tf_op jit(solution)/shard_map/ppermute | solution.py:521
  29.3 9.8 %collective-permute-start.3 = (f32[304,128]{1,0:T(8,128)S(1)}, f32[304,128]{1,0:T(8,128)S(1)}, u32[]{:S(2)}, u32[]{:S(2)}) collective-permute-start(f32[304,128]{1,0:T(8,128)S(1)} %get-tuple-element.25), channel_id=1, source_target_pairs={{1,2},{2,1},{3,4},{4,3},{5,6},{6,5},{9,10},{10,9},{11,12},{12,11},... | collective-permute-start | bytes 466952 | tf_op jit(solution)/shard_map/ppermute | solution.py:522
  34.2 4.9 %copy-start = (f32[2,65,8,128]{3,2,1,0:T(8,128)S(1)}, f32[2,65,8,128]{3,2,1,0:T(8,128)}, u32[]{:S(2)}) copy-start(f32[2,65,8,128]{3,2,1,0:T(8,128)} %param.15) | copy-start | bytes 1597444

commit v3 on v2

--- a/solution.py
+++ b/solution.py
@@ -4,6 +4,7 @@
 from jax.experimental import pallas as pl
 from jax.experimental.pallas import tpu as pltpu
 from jax.sharding import PartitionSpec as P
+
 
 STEPS = 4
 NT = 8
@@ -13,7 +14,8 @@
 SPLITS = 2
 NQ = 81
 NM = NQ // 3
-GROUP = 2
+MSG = NM * 8 + 16
+GROUP = 8
 PAY = 96 + 12 * 64 + 16
 TAB = 320 + 64 * SPLITS
 OWN = 8 * 64 + 16
@@ -112,7 +114,7 @@
             pay_b[start : start + 1, :] = jnp.where(odd, high, low)
 
 
-def scatter(jobs, hots, vals, tab, out_u, out_v):
+def scatter(jobs, tab, out_u, out_v):
     first = lax.broadcasted_iota(jnp.int32, (16, 128), 0).astype(F32)
     iota = [(first + 16.0 * b).astype(BF16) for b in range(8)]
     one = jnp.full((16, 128), 1, BF16)
@@ -129,7 +131,7 @@
         index.append(jnp.where((level == 64) & (row < ny), row.astype(F32), -1.0))
         index.append((cell & 127).astype(F32))
         for value in (wu, wv):
-            for s in range(SPLITS):
+            for _ in range(SPLITS):
                 top = value.astype(BF16).astype(F32)
                 value = value - top
                 index.append(top)
@@ -228,9 +230,9 @@
     ref[start + 16 : start + 24, :] = last
 
 
-def own_part(obs, kt, u, v, sw, sk, hot_a, hot_b, val_a, val_b, tab):
+def own_part(obs, kt, u, v, sw, sk, tab):
     job = (obs[0:32, :], obs[32:64, :], obs[64:96, :], 0, 8, 0)
-    scatter([job], (hot_a, hot_b), (val_a, val_b), tab, u, v)
+    scatter([job], tab, u, v)
     for y in range(8):
         for n, ref in enumerate((u, v)):
             strip(lambda t: wind_at(ref, None, y, t), sw, n * 8 + y)
@@ -250,8 +252,12 @@
     return tk, q * 7 + ((row + 4) if row < 0 else row - 4)
 
 
-def edges(pos, rec_a, rec_b, sw, sk, hu, hv, kh, tw, tk, msg_c, msg_d,
-          hot_a, hot_b, val_a, val_b, tab):
+def near(pos, rec_a, u, v, tab):
+    job = (rec_a[0:32, :], rec_a[32:64, :], rec_a[64:96, :], (pos[0] & 1) * 3, 5, 0)
+    scatter([job], tab, u, v)
+
+
+def edges(pos, rec_a, rec_b, au, av, sw, sk, hu, hv, kh, tw, tk, msg_c, msg_d, bu, bv, last, tab):
     odd = (pos[0] & 1) == 1
     for q in range(3):
         for j in range(7):
@@ -262,12 +268,11 @@
             src, dst = 864 + row * 3 + q, 1344 + j * 3 + q
             kh[dst : dst + 1, :] = jnp.where(odd, one[src : src + 1, :], two[src : src + 1, :])
     kh[1365:1368, :] = jnp.zeros((3, 128), F32)
-    jobs = []
-    for side in range(2):
-        one, two = (rec_a, rec_b) if side == 0 else (rec_b, rec_a)
-        part = jnp.where(odd, one[0:96, :], two[0:96, :])
-        jobs.append((part[0:32], part[32:64], part[64:96], 3 - 3 * side, 5, side * HALO))
-    scatter(jobs, (hot_a, hot_b), (val_a, val_b), tab, hu, hv)
+    job = (rec_b[0:32, :], rec_b[32:64, :], rec_b[64:96, :], 3 - (pos[0] & 1) * 3, 5, 0)
+    scatter([job], tab, bu, bv)
+    for out, one, two in ((hu, au, bu), (hv, av, bv)):
+        out[0:HALO, :] = jnp.where(odd, one[...], two[...])
+        out[HALO : 2 * HALO, :] = jnp.where(odd, two[...], one[...])
     for i in range(10):
         row = i - 5 if i < 5 else i + 3
         for n, ref in enumerate((hu, hv)):
@@ -284,19 +289,24 @@
             ref, index = strip_place(3 * i + t, sw, sk, tw, tk)
             left = ref[index * 24 : index * 24 + 8, :]
             packed.append((roll(left, 5 * t), roll(left, 5 * t - 5)))
-            row = NM * 8 + 3 * i + t
-            last = ref[index * 24 + 16 : index * 24 + 17, :]
-            msg_c[row : row + 1, :] = last
-            msg_d[row : row + 1, :] = last
+            row = 3 * i + t
+            last[row : row + 1, :] = ref[index * 24 + 16 : index * 24 + 17, :]
         right_edge, left_edge = (
             jnp.where(fifth < 6, packed[0][e], jnp.where(fifth < 11, packed[1][e], packed[2][e]))
             for e in range(2)
         )
         msg_c[i * 8 : i * 8 + 8, :] = jnp.where(odd_col, left_edge, right_edge)
         msg_d[i * 8 : i * 8 + 8, :] = jnp.where(odd_col, right_edge, left_edge)
-    fill = NM * 8 + NQ
-    for msg in (msg_c, msg_d):
-        msg[fill : fill + 7, :] = jnp.zeros((7, 128), F32)
+    last[NQ : NQ + 7, :] = jnp.zeros((7, 128), F32)
+    slot = lanes() // 16
+    for g in range(2):
+        packed = last[g * 64 : g * 64 + 8, :]
+        for k in range(1, 8 if g == 0 else 3):
+            start = g * 64 + k * 8
+            packed = jnp.where(slot == k, roll(last[start : start + 8, :], 16 * k), packed)
+        start = NM * 8 + g * 8
+        msg_c[start : start + 8, :] = packed
+        msg_d[start : start + 8, :] = packed
 
 
 def derive(wind, low, high, mask, put):
@@ -391,7 +401,7 @@
 
 
 def finish(
-    rows, columns, pos, rec_c, rec_d, sw, sk, tw, tk, main, norm, out, mw, mk, masks, fa, fb
+    rows, columns, pos, rec_c, rec_d, sw, sk, tw, tk, main, norm, out, mw, mk, masks, fa, fb, last_c, last_d
 ):
     low, high = ends(pos, rows)
     odd_col = (pos[1] & 1) == 1
@@ -401,14 +411,17 @@
     take_left = (fifth >= 1) & (fifth <= 5)
     take_right = (fifth >= 6) & (fifth <= 10)
     take_last = (take_left & (sub == 0)) | (take_right & (sub == 1))
+    for rec, unpacked in ((rec_c, last_c), (rec_d, last_d)):
+        for k in range(11):
+            start = NM * 8 + k // 8 * 8
+            unpacked[k * 8 : k * 8 + 8, :] = roll(rec[start : start + 8, :], -16 * (k % 8))
     for k in range(NQ):
         i, t = k // 3, k % 3
         a = rec_c[i * 8 : i * 8 + 8, :]
         b = rec_d[i * 8 : i * 8 + 8, :]
         from_left = roll(jnp.where(odd_col, a, b), -5 * t)
         from_right = roll(jnp.where(odd_col, b, a), 5 - 5 * t)
-        row = NM * 8 + k
-        last = jnp.where((sub == 0) == odd_col, wide(rec_c, row), wide(rec_d, row))
+        last = jnp.where((sub == 0) == odd_col, wide(last_c, k), wide(last_d, k))
         src, index = strip_place(k, sw, sk, tw, tk)
         here = index * 24
         dst, start = (mw, k * 24) if k < 36 else (mk, (k - 36) * 24)
@@ -498,13 +511,7 @@
     )
     rec_b = lax.ppermute(pay_b, "row", pairs(rows, 1))
     rec_a = lax.ppermute(pay_a, "row", pairs(rows, 0))
-    work = (
-        pltpu.VMEM((KC // 128, OWN, 128), BF16),
-        pltpu.VMEM((KC // 128, OWN, 128), BF16),
-        pltpu.VMEM((KC // 128, 256 * SPLITS, 128), BF16),
-        pltpu.VMEM((KC // 128, 256 * SPLITS, 128), BF16),
-        pltpu.VMEM((2 * TAB, 128), F32),
-    )
+    work = buffers((TAB, F32))
     u, v, sw, sk = call(
         own_part,
         (OWN, OWN, 16 * 24, 24 * 24),
@@ -512,12 +519,15 @@
         work,
         estimate(3_000_000_000, 2_000_000),
     )(pay_a[0:96], kt)
+    au, av = call(
+        near, (HALO, HALO), [SM, VM], work, estimate(3_000_000_000, 2_000_000)
+    )(pos, rec_a)
     hu, hv, kh, tw, tk, msg_c, msg_d = call(
         edges,
-        (2 * HALO, 2 * HALO, 21 * 64 + 24, 20 * 24, 21 * 24, NM * 8 + 88, NM * 8 + 88),
-        [SM] + [VM] * 4,
-        work,
-    )(pos, rec_a, rec_b, sw, sk)
+        (2 * HALO, 2 * HALO, 21 * 64 + 24, 20 * 24, 21 * 24, MSG, MSG),
+        [SM] + [VM] * 6,
+        buffers((HALO, F32), (HALO, F32), (88, F32)) + work,
+    )(pos, rec_a, rec_b, au, av, sw, sk)
     rec_c = lax.ppermute(msg_c, "col", pairs(columns, 0))
     rec_d = lax.ppermute(msg_d, "col", pairs(columns, 1))
     (main,) = call(
@@ -531,7 +541,7 @@
         lambda *refs: finish(rows, columns, *refs),
         (2 * 65 * 8,),
         [SM] + [VM] * 8,
-        buffers((36 * 24, F32), (45 * 24, F32), (24, F32), (32 * 24, F32), (32 * 24, F32)),
+        buffers((36 * 24, F32), (45 * 24, F32), (24, F32), (32 * 24, F32), (32 * 24, F32), (88, F32), (88, F32)),
     )(pos, rec_c, rec_d, sw, sk, tw, tk, main, flat(norm_scale))
     return out.reshape(norm_scale.shape)
 

time: 42.1 us -> 41.6 us (0.988)
  the two profiles are of different devices: /device:TPU:30 before, /device:TPU:38 now
where the time goes in v3:
time: 41.6 us; the launch traced here: 41.3 us
  starting transfers between devices  21.6 us (52%)
  Pallas kernels  14.8 us (36%)
  waiting for transfers between devices  4.09 us (10%)
  between operations  0.74 us (2%)
    ppermute x1, starting transfers between devices, on_device(): rec_b = lax.ppermute(pay_b, 'row', pairs(rows, 1))  15 us
    pallas_call x1, Pallas kernels, on_device(): call(lambda *refs: middle(rows, *refs), (16 * 64,), [SM] + [VM] * 6, buff...  2.99 us
    ppermute x1, waiting for transfers between devices, on_device(): rec_d = lax.ppermute(msg_d, 'col', pairs(columns, 1))  2.79 us
    pallas_call x1, Pallas kernels, on_device(): call(lambda *refs: finish(rows, columns, *refs), (2 * 65 * 8,), [SM] + [V...  2.66 us
    ppermute x1, starting transfers between devices, on_device(): rec_c = lax.ppermute(msg_c, 'col', pairs(columns, 0))  2.58 us
    pallas_call x1, Pallas kernels, on_device(): call(own_part, (OWN, OWN, 16 * 24, 24 * 24), [VM] * 2, work, estimate(300...  2.55 us
    pallas_call x1, Pallas kernels, on_device(): call(edges, (2 * HALO, 2 * HALO, 21 * 64 + 24, 20 * 24, 21 * 24, MSG, MSG...  2.49 us
    pallas_call x1, Pallas kernels, on_device(): call(near, (HALO, HALO), [SM, VM], work, estimate(3000000000, 2000000))  2.17 us
  transfers between devices with their start and end apart: 4, of which 2 were waited for; matrix products, arithmetic and copies ran while one was open for 0% of the time, Pallas kernels for 19%

profile of v3, /device:TPU:38, one launch (start us, length us, event | category | flops | bytes accessed | tf_op | source)
XLA Modules:
  0.0 41.3 jit_solution(15841794638950200272)
XLA Ops:
  0.7 0.1 pad_add_fusion.pos.refs_0_
  0.7 1.9 %shard_map.82 = (f32[880,128]{1,0:T(8,128)S(1)}, f32[880,128]{1,0:T(8,128)S(1)}, f32[1560,128]{1,0:T(8,128)S(1)}) custom-call(s32[2]{0:T(128)S(1)} %pad_add_fusion.pos.refs_0_, s32[1,1]{1,0:T(1,128)S(6)} %copy.9.gate, f32[32,128]{1,0:T(8,128)} %bitcast.14, s32[32,128]{1,0:T(8,128)} %bitcast.15, f32[32,128]{1,0:T(8,128)} %bitcast.16, f32[520,128]{1,0:T(8,128)} %bitcast.11, ...), custom_call_target="tpu_custom_call" | custom-call | tf_op jit(solution)/shard_map/pallas_call | solution.py:498
  2.7 1.9 %collective-permute-start = (f32[880,128]{1,0:T(8,128)S(1)}, f32[880,128]{1,0:T(8,128)S(1)}, u32[]{:S(2)}, u32[]{:S(2)}) collective-permute-start(f32[880,128]{1,0:T(8,128)S(1)} %get-tuple-element.21), channel_id=1, source_target_pairs={{0,8},{8,0},{16,24},{24,16},{32,40},{40,32},{48,56},{56,48},{64,72... | collective-permute-start | bytes 1351688 | tf_op jit(solution)/shard_map/ppermute | solution.py:513
  4.6 15.0 %collective-permute-start.1 = (f32[880,128]{1,0:T(8,128)S(1)}, f32[880,128]{1,0:T(8,128)S(1)}, u32[]{:S(2)}, u32[]{:S(2)}) collective-permute-start(f32[880,128]{1,0:T(8,128)S(1)} %get-tuple-element.22), channel_id=1, source_target_pairs={{8,16},{16,8},{24,32},{32,24},{40,48},{48,40},{56,64},{64,56},{72,... | collective-permute-start | bytes 1351688 | tf_op jit(solution)/shard_map/ppermute | solution.py:512
  19.6 2.6 %shard_map.84 = (f32[528,128]{1,0:T(8,128)S(1)}, f32[528,128]{1,0:T(8,128)S(1)}, f32[384,128]{1,0:T(8,128)S(1)}, f32[576,128]{1,0:T(8,128)S(1)}) custom-call(f32[96,128]{1,0:T(8,128)S(1)} %slice.3.obs, f32[1560,128]{1,0:T(8,128)S(1)} %get-tuple-element.25.kt.refs_5_), custom_call_target="tpu_custom_call" | custom-call | flops 3000000000 | bytes 2000000 | tf_op jit(solution)/shard_map/pallas_call | solution.py:515
  22.1 0.0 collective-permute-done.rec_a
  22.1 2.2 %shard_map.83 = (f32[336,128]{1,0:T(8,128)S(1)}, f32[336,128]{1,0:T(8,128)S(1)}) custom-call(s32[2]{0:T(128)S(1)} %pad_add_fusion.pos.refs_0_, f32[880,128]{1,0:T(8,128)S(1)} %collective-permute-done.rec_a), custom_call_target="tpu_custom_call" | custom-call | flops 3000000000 | bytes 2000000 | tf_op jit(solution)/shard_map/pallas_call | solution.py:522
  24.3 1.3 %collective-permute-done.1.rec_b = f32[880,128]{1,0:T(8,128)S(1)} collective-permute-done((f32[880,128]{1,0:T(8,128)S(1)}, f32[880,128]{1,0:T(8,128)S(1)}, u32[]{:S(2)}, u32[]{:S(2)}) %collective-permute-start.1) | collective-permute-done | bytes 450592 | tf_op jit(solution)/shard_map/ppermute | solution.py:512
  25.6 2.5 %shard_map.85 = (f32[672,128]{1,0:T(8,128)S(1)}, f32[672,128]{1,0:T(8,128)S(1)}, f32[1368,128]{1,0:T(8,128)S(1)}, f32[480,128]{1,0:T(8,128)S(1)}, f32[504,128]{1...) custom-call(s32[2]{0:T(128)S(1)} %pad_add_fusion.pos.refs_0_, ...), custom_call_target="tpu_custom_call" | custom-call | tf_op jit(solution)/shard_map/pallas_call | solution.py:525
  28.1 2.6 %collective-permute-start.2 = (f32[232,128]{1,0:T(8,128)S(1)}, f32[232,128]{1,0:T(8,128)S(1)}, u32[]{:S(2)}, u32[]{:S(2)}) collective-permute-start(f32[232,128]{1,0:T(8,128)S(1)} %get-tuple-element.28), channel_id=1, source_target_pairs={{0,1},{1,0},{2,3},{3,2},{4,5},{5,4},{6,7},{7,6},{8,9},{9,8},{10,11... | collective-permute-start | bytes 356360 | tf_op jit(solution)/shard_map/ppermute | solution.py:531
  30.7 2.1 %collective-permute-start.3 = (f32[232,128]{1,0:T(8,128)S(1)}, f32[232,128]{1,0:T(8,128)S(1)}, u32[]{:S(2)}, u32[]{:S(2)}) collective-permute-start(f32[232,128]{1,0:T(8,128)S(1)} %get-tuple-element.29), channel_id=1, source_target_pairs={{1,2},{2,1},{3,4},{4,3},{5,6},{6,5},{9,10},{10,9},{11,12},{12,11},... | collective-permute-start | bytes 356360 | tf_op jit(solution)/shard_map/ppermute | solution.py:532
  32.8 0.0 copy-start
  32.8 3.0 %shard_map.86.refs_7_ = f32[1024,128]{1,0:T(8,128)S(1)} custom-call(s32[2]{0:T(128)S(1)} %pad_add_fusion.pos.refs_0_, f32[528,128]{1,0:T(8,128)S(1)} %get-tuple-element.32.refs_1_, f32[528,128]{1,0:T(8,128)S(1)} %get-tuple-element.33.refs_2_, f32[672,128]{1,0:T(8,128)S(1)} %get-tuple-element.34.refs_3_, f32[672,128]{1,0:T(8,128)S(1)} %get-tuple-element.35.refs_4_, ...), custom_call_target="tpu_custom_call" | custom-call | flops 3000000000 | bytes 4000000 | tf_op jit(solution)/shard_map/pallas_call | solution.py:533
  35.8 0.0 collective-permute-done.2.refs_1_
  35.9 2.8 %collective-permute-done.3.refs_2_ = f32[232,128]{1,0:T(8,128)S(1)} collective-permute-done((f32[232,128]{1,0:T(8,128)S(1)}, f32[232,128]{1,0:T(8,128)S(1)}, u32[]{:S(2)}, u32[]{:S(2)}) %collective-permute-start.3) | collective-permute-done | bytes 118816 | tf_op jit(solution)/shard_map/ppermute | solution.py:532
  38.6 0.0 copy-done
  38.6 2.7 %shard_map.87 = f32[1040,128]{1,0:T(8,128)} custom-call(s32[2]{0:T(128)S(1)} %pad_add_fusion.pos.refs_0_, f32[232,128]{1,0:T(8,128)S(1)} %collective-permute-done.2.refs_1_, f32[232,128]{1,0:T(8,128)S(1)} %collective-permute-done.3.refs_2_, f32[384,128]{1,0:T(8,128)S(1)} %get-tuple-element.26.sw.refs_3_, f32[576,128]{1,0:T(8,128)S(1)} %get-tuple-element.27.sk.refs_4_, ...), custom_call_target="tpu_custom_call" | custom-call | tf_op jit(solution)/shard_map/pallas_call | solution.py:540
  (1 shorter events, 0.0 us)
Async XLA Ops:
  2.7 19.5 %collective-permute-start = (f32[880,128]{1,0:T(8,128)S(1)}, f32[880,128]{1,0:T(8,128)S(1)}, u32[]{:S(2)}, u32[]{:S(2)}) collective-permute-start(f32[880,128]{1,0:T(8,128)S(1)} %get-tuple-element.21), channel_id=1, source_target_pairs={{0,8},{8,0},{16,24},{24,16},{32,40},{40,32},{48,56},{56,48},{64,72... | collective-permute-start | bytes 1351688 | tf_op jit(solution)/shard_map/ppermute | solution.py:513
  4.6 21.0 %collective-permute-start.1 = (f32[880,128]{1,0:T(8,128)S(1)}, f32[880,128]{1,0:T(8,128)S(1)}, u32[]{:S(2)}, u32[]{:S(2)}) collective-permute-start(f32[880,128]{1,0:T(8,128)S(1)} %get-tuple-element.22), channel_id=1, source_target_pairs={{8,16},{16,8},{24,32},{32,24},{40,48},{48,40},{56,64},{64,56},{72,... | collective-permute-start | bytes 1351688 | tf_op jit(solution)/shard_map/ppermute | solution.py:512
  28.1 7.7 %collective-permute-start.2 = (f32[232,128]{1,0:T(8,128)S(1)}, f32[232,128]{1,0:T(8,128)S(1)}, u32[]{:S(2)}, u32[]{:S(2)}) collective-permute-start(f32[232,128]{1,0:T(8,128)S(1)} %get-tuple-element.28), channel_id=1, source_target_pairs={{0,1},{1,0},{2,3},{3,2},{4,5},{5,4},{6,7},{7,6},{8,9},{9,8},{10,11... | collective-permute-start | bytes 356360 | tf_op jit(solution)/shard_map/ppermute | solution.py:531
  30.7 7.9 %collective-permute-start.3 = (f32[232,128]{1,0:T(8,128)S(1)}, f32[232,128]{1,0:T(8,128)S(1)}, u32[]{:S(2)}, u32[]{:S(2)}) collective-permute-start(f32[232,128]{1,0:T(8,128)S(1)} %get-tuple-element.29), channel_id=1, source_target_pairs={{1,2},{2,1},{3,4},{4,3},{5,6},{6,5},{9,10},{10,9},{11,12},{12,11},... | collective-permute-start | bytes 356360 | tf_op jit(solution)/shard_map/ppermute | solution.py:532
  32.8 5.8 %copy-start = (f32[2,65,8,128]{3,2,1,0:T(8,128)S(1)}, f32[2,65,8,128]{3,2,1,0:T(8,128)}, u32[]{:S(2)}) copy-start(f32[2,65,8,128]{3,2,1,0:T(8,128)} %param.15) | copy-start | bytes 1597444

commit v4 on v3

--- a/solution.py
+++ b/solution.py
@@ -13,10 +13,17 @@
 KC = 1024
 SPLITS = 2
 NQ = 81
-NM = NQ // 3
+GROUPS = [(list(range(k, k + 3)), 5) for k in range(0, 36, 3)]
+GROUPS += [(list(range(k, k + 4)), 4) for k in range(37, NQ, 4)]
+NM = len(GROUPS)
 MSG = NM * 8 + 16
 GROUP = 8
-PAY = 96 + 12 * 64 + 16
+HIGH = [(row, q) for row in range(4, 8) for q in range(3)][1:]
+LOW = [(row, q) for row in range(4) for q in range(3)][: len(HIGH)]
+UNITS = len(HIGH)
+TAIL = 96 + UNITS * 64
+PAY = TAIL + 16
+PIECES = 4
 TAB = 320 + 64 * SPLITS
 OWN = 8 * 64 + 16
 HALO = 5 * 64 + 16
@@ -56,24 +63,25 @@
 def prepare(pos, gate, resid_h, cell_h, azimuth_h, kxx_h, kyy_h, ksh_h, pay_a, pay_b, kt,
             resid, cell, azimuth, kxx, kyy, ksh, sems):
     copies = []
-    for i, (src, dst) in enumerate(
-        (
-            (resid_h, resid),
-            (cell_h, cell),
-            (azimuth_h, azimuth),
-            (kxx_h, kxx),
-            (kyy_h, kyy),
-            (ksh_h, ksh),
-        )
-    ):
-        copies.append(pltpu.make_async_copy(src, dst, sems.at[i]))
+
+    def copy(src, dst):
+        copies.append(pltpu.make_async_copy(src, dst, sems.at[len(copies)]))
         copies[-1].start()
+
+    for src, dst in ((resid_h, resid), (cell_h, cell), (azimuth_h, azimuth)):
+        copy(src, dst)
+    tensors = ((kxx_h, kxx), (kyy_h, kyy), (ksh_h, ksh))
+    size = 512 // PIECES
+    for piece in range(PIECES):
+        span = slice(piece * size, 520 if piece == PIECES - 1 else (piece + 1) * size)
+        for src, dst in tensors:
+            copy(src.at[span, :], dst.at[span, :])
     odd = (pos[0] & 1) == 1
     slot = lax.broadcasted_iota(jnp.int32, (32, 128), 0) * 128 + lax.broadcasted_iota(
         jnp.int32, (32, 128), 1
     )
-    for copy in copies[:3]:
-        copy.wait()
+    for ready in copies[:3]:
+        ready.wait()
     weight = jnp.where(slot < gate[0, 0], resid[...], 0.0)
     angle = azimuth[...]
     wu = weight * jnp.sin(angle)
@@ -83,35 +91,35 @@
         pay[0:32, :] = wu
         pay[32:64, :] = wv
         pay[64:96, :] = cf
-        pay[876:880, :] = jnp.zeros((4, 128), F32)
-    for copy in copies[3:]:
-        copy.wait()
+        pay[TAIL + UNITS : PAY, :] = jnp.zeros((PAY - TAIL - UNITS, 128), F32)
 
     def entries(get):
         xx, yy = get(kxx), get(kyy)
         return xx, get(ksh) * jnp.sqrt(xx * yy), yy
 
-    for tile in range(NT):
-        rows = []
-        for y in range(8):
-            rows.append(entries(lambda ref: ref[pl.ds(tile * 64 + y, 8, stride=8), :]))
-            for q in range(3):
-                start = (q * 8 + y) * 64 + tile * 8
-                kt[start : start + 8, :] = rows[y][q]
-        for i in range(4):
-            for q in range(3):
-                start = 96 + (i * 3 + q) * 64 + tile * 8
-                low, high = rows[i][q], rows[i + 4][q]
+    for piece in range(PIECES):
+        for ready in copies[3 + 3 * piece : 6 + 3 * piece]:
+            ready.wait()
+        for tile in range(piece * NT // PIECES, (piece + 1) * NT // PIECES):
+            rows = []
+            for y in range(8):
+                rows.append(entries(lambda ref: ref[pl.ds(tile * 64 + y, 8, stride=8), :]))
+                for q in range(3):
+                    start = (q * 8 + y) * 64 + tile * 8
+                    kt[start : start + 8, :] = rows[y][q]
+            for k in range(UNITS):
+                start = 96 + k * 64 + tile * 8
+                low, high = rows[LOW[k][0]][LOW[k][1]], rows[HIGH[k][0]][HIGH[k][1]]
                 pay_a[start : start + 8, :] = jnp.where(odd, low, high)
                 pay_b[start : start + 8, :] = jnp.where(odd, high, low)
     last = entries(lambda ref: ref[512:520, :])
     for q in range(3):
         kt[1536 + q * 8 : 1544 + q * 8, :] = last[q]
-        for i in range(4):
-            start = 864 + i * 3 + q
-            low, high = last[q][i : i + 1, :], last[q][i + 4 : i + 5, :]
-            pay_a[start : start + 1, :] = jnp.where(odd, low, high)
-            pay_b[start : start + 1, :] = jnp.where(odd, high, low)
+    for k in range(UNITS):
+        start = TAIL + k
+        low, high = (last[q][y : y + 1, :] for y, q in (LOW[k], HIGH[k]))
+        pay_a[start : start + 1, :] = jnp.where(odd, low, high)
+        pay_b[start : start + 1, :] = jnp.where(odd, high, low)
 
 
 def scatter(jobs, tab, out_u, out_v):
@@ -252,6 +260,11 @@
     return tk, q * 7 + ((row + 4) if row < 0 else row - 4)
 
 
+def message_rolls(t, width):
+    place = width * t + (1 if width == 5 else 0)
+    return place - (6 - width), place - 6
+
+
 def near(pos, rec_a, u, v, tab):
     job = (rec_a[0:32, :], rec_a[32:64, :], rec_a[64:96, :], (pos[0] & 1) * 3, 5, 0)
     scatter([job], tab, u, v)
@@ -261,12 +274,17 @@
     odd = (pos[0] & 1) == 1
     for q in range(3):
         for j in range(7):
-            row, one, two = (j, rec_a, rec_b) if j < 4 else (j - 4, rec_b, rec_a)
-            src = 96 + (row * 3 + q) * 64
-            dst = (j * 3 + q) * 64
-            kh[dst : dst + 64, :] = jnp.where(odd, one[src : src + 64, :], two[src : src + 64, :])
-            src, dst = 864 + row * 3 + q, 1344 + j * 3 + q
-            kh[dst : dst + 1, :] = jnp.where(odd, one[src : src + 1, :], two[src : src + 1, :])
+            dst, tail = (j * 3 + q) * 64, 1344 + j * 3 + q
+            if j < 4 and (j + 4, q) not in HIGH:
+                kh[dst : dst + 64, :] = jnp.zeros((64, 128), F32)
+                kh[tail : tail + 1, :] = jnp.zeros((1, 128), F32)
+                continue
+            k = HIGH.index((j + 4, q)) if j < 4 else LOW.index((j - 4, q))
+            one, two = (rec_a, rec_b) if j < 4 else (rec_b, rec_a)
+            src = slice(96 + k * 64, 96 + k * 64 + 64)
+            kh[dst : dst + 64, :] = jnp.where(odd, one[src, :], two[src, :])
+            src = slice(TAIL + k, TAIL + k + 1)
+            kh[tail : tail + 1, :] = jnp.where(odd, one[src, :], two[src, :])
     kh[1365:1368, :] = jnp.zeros((3, 128), F32)
     job = (rec_b[0:32, :], rec_b[32:64, :], rec_b[64:96, :], 3 - (pos[0] & 1) * 3, 5, 0)
     scatter([job], tab, bu, bv)
@@ -283,20 +301,22 @@
             strip(lambda t: kappa_at(None, kh, q, row, t), tk, q * 7 + i)
     fifth = lanes() % 16
     odd_col = (pos[1] & 1) == 1
-    for i in range(NM):
+    for i, (members, width) in enumerate(GROUPS):
         packed = []
-        for t in range(3):
-            ref, index = strip_place(3 * i + t, sw, sk, tw, tk)
+        for t, k in enumerate(members):
+            ref, index = strip_place(k, sw, sk, tw, tk)
             left = ref[index * 24 : index * 24 + 8, :]
-            packed.append((roll(left, 5 * t), roll(left, 5 * t - 5)))
-            row = 3 * i + t
-            last[row : row + 1, :] = ref[index * 24 + 16 : index * 24 + 17, :]
-        right_edge, left_edge = (
-            jnp.where(fifth < 6, packed[0][e], jnp.where(fifth < 11, packed[1][e], packed[2][e]))
-            for e in range(2)
-        )
+            packed.append([roll(left, by) for by in message_rolls(t, width)])
+        right_edge, left_edge = packed[-1]
+        for t in range(len(members) - 1, 0, -1):
+            before = fifth < width * t + (1 if width == 5 else 0)
+            right_edge = jnp.where(before, packed[t - 1][0], right_edge)
+            left_edge = jnp.where(before, packed[t - 1][1], left_edge)
         msg_c[i * 8 : i * 8 + 8, :] = jnp.where(odd_col, left_edge, right_edge)
         msg_d[i * 8 : i * 8 + 8, :] = jnp.where(odd_col, right_edge, left_edge)
+    for k in range(NQ):
+        ref, index = strip_place(k, sw, sk, tw, tk)
+        last[k : k + 1, :] = ref[index * 24 + 16 : index * 24 + 17, :]
     last[NQ : NQ + 7, :] = jnp.zeros((7, 128), F32)
     slot = lanes() // 16
     for g in range(2):
@@ -401,7 +421,7 @@
 
 
 def finish(
-    rows, columns, pos, rec_c, rec_d, sw, sk, tw, tk, main, norm, out, mw, mk, masks, fa, fb, last_c, last_d
+    rows, columns, pos, rec_c, rec_d, sw, sk, tw, tk, main, norm, result, mw, mk, masks, fa, fb, last_c, last_d, out, sems
 ):
     low, high = ends(pos, rows)
     odd_col = (pos[1] & 1) == 1
@@ -415,20 +435,31 @@
         for k in range(11):
             start = NM * 8 + k // 8 * 8
             unpacked[k * 8 : k * 8 + 8, :] = roll(rec[start : start + 8, :], -16 * (k % 8))
+    take = {}
+    for width in (5, 4):
+        take[width] = (
+            (fifth >= 6 - width) & (fifth <= 5),
+            (fifth >= 6) & (fifth <= 5 + width),
+        )
+    place = {}
+    for i, (members, width) in enumerate(GROUPS):
+        for t, k in enumerate(members):
+            place[k] = i, t, width
     for k in range(NQ):
-        i, t = k // 3, k % 3
-        a = rec_c[i * 8 : i * 8 + 8, :]
-        b = rec_d[i * 8 : i * 8 + 8, :]
-        from_left = roll(jnp.where(odd_col, a, b), -5 * t)
-        from_right = roll(jnp.where(odd_col, b, a), 5 - 5 * t)
-        last = jnp.where((sub == 0) == odd_col, wide(last_c, k), wide(last_d, k))
         src, index = strip_place(k, sw, sk, tw, tk)
         here = index * 24
+        left, right = src[here : here + 8, :], src[here + 8 : here + 16, :]
+        if k in place:
+            i, t, width = place[k]
+            a = rec_c[i * 8 : i * 8 + 8, :]
+            b = rec_d[i * 8 : i * 8 + 8, :]
+            right_by, left_by = message_rolls(t, width)
+            left = jnp.where(take[width][0], roll(jnp.where(odd_col, a, b), -right_by), left)
+            right = jnp.where(take[width][1], roll(jnp.where(odd_col, b, a), -left_by), right)
+        last = jnp.where((sub == 0) == odd_col, wide(last_c, k), wide(last_d, k))
         dst, start = (mw, k * 24) if k < 36 else (mk, (k - 36) * 24)
-        dst[start : start + 8, :] = jnp.where(take_left, from_left, src[here : here + 8, :])
-        dst[start + 8 : start + 16, :] = jnp.where(
-            take_right, from_right, src[here + 8 : here + 16, :]
-        )
+        dst[start : start + 8, :] = left
+        dst[start + 8 : start + 16, :] = right
         dst[start + 16 : start + 24, :] = jnp.where(take_last, last, src[here + 16 : here + 24, :])
     west = jnp.where(pos[1] == 0, 0.0, 1.0).astype(F32)
     east = jnp.where(pos[1] == columns - 1, 0.0, 1.0).astype(F32)
@@ -457,6 +488,7 @@
                 )
     done = fb if STEPS % 2 == 1 else fa
     edge = (lane < 5) | (lane >= 123)
+    copies = []
     for n in range(2):
         for y in range(8):
             left, right, last = (slab(done, 3, tile)[0](n, y) for tile in range(3))
@@ -470,14 +502,19 @@
             value = jnp.where(edge[0:1], both, last[2:3])
             spot = n * 520 + 512 + y
             out[spot : spot + 1, :] = norm[spot : spot + 1, :] * value
-
-
-def call(body, shapes, specs, scratch=(), cost=None):
+        half = pl.ds(n * 520, 520)
+        copies.append(pltpu.make_async_copy(out.at[half, :], result.at[half, :], sems.at[n]))
+        copies[-1].start()
+    for copy in copies:
+        copy.wait()
+
+
+def call(body, shapes, specs, scratch=(), cost=None, out_spec=VM):
     return pl.pallas_call(
         body,
         out_shape=[jax.ShapeDtypeStruct((n, 128), F32) for n in shapes],
         in_specs=specs,
-        out_specs=[VM] * len(shapes),
+        out_specs=[out_spec] * len(shapes),
         scratch_shapes=list(scratch),
         cost_estimate=cost,
         compiler_params=pltpu.CompilerParams(vmem_limit_bytes=32 << 20),
@@ -500,7 +537,7 @@
         (PAY, PAY, 24 * 64 + 24),
         [SM, SM] + [HB] * 6,
         buffers((32, F32), (32, jnp.int32), (32, F32), (520, F32), (520, F32), (520, F32))
-        + (pltpu.SemaphoreType.DMA((6,)),),
+        + (pltpu.SemaphoreType.DMA((3 + 3 * PIECES,)),),
     )(
         pos,
         gate_count,
@@ -541,7 +578,9 @@
         lambda *refs: finish(rows, columns, *refs),
         (2 * 65 * 8,),
         [SM] + [VM] * 8,
-        buffers((36 * 24, F32), (45 * 24, F32), (24, F32), (32 * 24, F32), (32 * 24, F32), (88, F32), (88, F32)),
+        buffers((36 * 24, F32), (45 * 24, F32), (24, F32), (32 * 24, F32), (32 * 24, F32), (88, F32), (88, F32), (1040, F32))
+        + (pltpu.SemaphoreType.DMA((2,)),),
+        out_spec=HB,
     )(pos, rec_c, rec_d, sw, sk, tw, tk, main, flat(norm_scale))
     return out.reshape(norm_scale.shape)
 

time: 41.6 us -> 41.1 us (0.988)
  waiting for transfers between devices: 4.09 us -> 3.54 us
where the time goes in v4:
time: 41.1 us; the launch traced here: 40.8 us
  starting transfers between devices  21.6 us (53%)
  Pallas kernels  14.8 us (36%)
  waiting for transfers between devices  3.54 us (9%)
  between operations  0.74 us (2%)
    ppermute x1, starting transfers between devices, on_device(): rec_b = lax.ppermute(pay_b, 'row', pairs(rows, 1))  15 us
    pallas_call x1, Pallas kernels, on_device(): call(lambda *refs: middle(rows, *refs), (16 * 64,), [SM] + [VM] * 6, buff...  3 us
    pallas_call x1, Pallas kernels, on_device(): call(lambda *refs: finish(rows, columns, *refs), (2 * 65 * 8,), [SM] + [V...  2.62 us
    ppermute x1, waiting for transfers between devices, on_device(): rec_d = lax.ppermute(msg_d, 'col', pairs(columns, 1))  2.59 us
    ppermute x1, starting transfers between devices, on_device(): rec_c = lax.ppermute(msg_c, 'col', pairs(columns, 0))  2.58 us
    pallas_call x1, Pallas kernels, on_device(): call(own_part, (OWN, OWN, 16 * 24, 24 * 24), [VM] * 2, work, estimate(300...  2.56 us
    pallas_call x1, Pallas kernels, on_device(): call(edges, (2 * HALO, 2 * HALO, 21 * 64 + 24, 20 * 24, 21 * 24, MSG, MSG...  2.49 us
    pallas_call x1, Pallas kernels, on_device(): call(near, (HALO, HALO), [SM, VM], work, estimate(3000000000, 2000000))  2.17 us
  transfers between devices with their start and end apart: 4, of which 2 were waited for; matrix products, arithmetic and copies ran while one was open for 0% of the time, Pallas kernels for 19%

profile of v4, /device:TPU:38, one launch (start us, length us, event | category | flops | bytes accessed | tf_op | source)
XLA Modules:
  0.0 40.8 jit_solution(10364982470437913849)
XLA Ops:
  0.7 0.1 pad_add_fusion.pos.refs_0_
  0.7 2.0 %shard_map.82 = (f32[816,128]{1,0:T(8,128)S(1)}, f32[816,128]{1,0:T(8,128)S(1)}, f32[1560,128]{1,0:T(8,128)S(1)}) custom-call(s32[2]{0:T(128)S(1)} %pad_add_fusion.pos.refs_0_, s32[1,1]{1,0:T(1,128)S(6)} %copy.9.gate, f32[32,128]{1,0:T(8,128)} %bitcast.14, s32[32,128]{1,0:T(8,128)} %bitcast.15, f32[32,128]{1,0:T(8,128)} %bitcast.16, f32[520,128]{1,0:T(8,128)} %bitcast.11, ...), custom_call_target="tpu_custom_call" | custom-call | tf_op jit(solution)/shard_map/pallas_call | solution.py:535
  2.7 1.9 %collective-permute-start = (f32[816,128]{1,0:T(8,128)S(1)}, f32[816,128]{1,0:T(8,128)S(1)}, u32[]{:S(2)}, u32[]{:S(2)}) collective-permute-start(f32[816,128]{1,0:T(8,128)S(1)} %get-tuple-element.21), channel_id=1, source_target_pairs={{0,8},{8,0},{16,24},{24,16},{32,40},{40,32},{48,56},{56,48},{64,72... | collective-permute-start | bytes 1253384 | tf_op jit(solution)/shard_map/ppermute | solution.py:550
  4.6 15.0 %collective-permute-start.1 = (f32[816,128]{1,0:T(8,128)S(1)}, f32[816,128]{1,0:T(8,128)S(1)}, u32[]{:S(2)}, u32[]{:S(2)}) collective-permute-start(f32[816,128]{1,0:T(8,128)S(1)} %get-tuple-element.22), channel_id=1, source_target_pairs={{8,16},{16,8},{24,32},{32,24},{40,48},{48,40},{56,64},{64,56},{72,... | collective-permute-start | bytes 1253384 | tf_op jit(solution)/shard_map/ppermute | solution.py:549
  19.6 2.6 %shard_map.84 = (f32[528,128]{1,0:T(8,128)S(1)}, f32[528,128]{1,0:T(8,128)S(1)}, f32[384,128]{1,0:T(8,128)S(1)}, f32[576,128]{1,0:T(8,128)S(1)}) custom-call(f32[96,128]{1,0:T(8,128)S(1)} %slice.3.obs, f32[1560,128]{1,0:T(8,128)S(1)} %get-tuple-element.25.kt.refs_5_), custom_call_target="tpu_custom_call" | custom-call | flops 3000000000 | bytes 2000000 | tf_op jit(solution)/shard_map/pallas_call | solution.py:552
  22.2 0.0 collective-permute-done.rec_a
  22.2 2.2 %shard_map.83 = (f32[336,128]{1,0:T(8,128)S(1)}, f32[336,128]{1,0:T(8,128)S(1)}) custom-call(s32[2]{0:T(128)S(1)} %pad_add_fusion.pos.refs_0_, f32[816,128]{1,0:T(8,128)S(1)} %collective-permute-done.rec_a), custom_call_target="tpu_custom_call" | custom-call | flops 3000000000 | bytes 2000000 | tf_op jit(solution)/shard_map/pallas_call | solution.py:559
  24.4 0.9 %collective-permute-done.1.rec_b = f32[816,128]{1,0:T(8,128)S(1)} collective-permute-done((f32[816,128]{1,0:T(8,128)S(1)}, f32[816,128]{1,0:T(8,128)S(1)}, u32[]{:S(2)}, u32[]{:S(2)}) %collective-permute-start.1) | collective-permute-done | bytes 417824 | tf_op jit(solution)/shard_map/ppermute | solution.py:549
  25.3 2.5 %shard_map.85 = (f32[672,128]{1,0:T(8,128)S(1)}, f32[672,128]{1,0:T(8,128)S(1)}, f32[1368,128]{1,0:T(8,128)S(1)}, f32[480,128]{1,0:T(8,128)S(1)}, f32[504,128]{1...) custom-call(s32[2]{0:T(128)S(1)} %pad_add_fusion.pos.refs_0_, ...), custom_call_target="tpu_custom_call" | custom-call | tf_op jit(solution)/shard_map/pallas_call | solution.py:562
  27.8 2.6 %collective-permute-start.2 = (f32[200,128]{1,0:T(8,128)S(1)}, f32[200,128]{1,0:T(8,128)S(1)}, u32[]{:S(2)}, u32[]{:S(2)}) collective-permute-start(f32[200,128]{1,0:T(8,128)S(1)} %get-tuple-element.28), channel_id=1, source_target_pairs={{0,1},{1,0},{2,3},{3,2},{4,5},{5,4},{6,7},{7,6},{8,9},{9,8},{10,11... | collective-permute-start | bytes 307208 | tf_op jit(solution)/shard_map/ppermute | solution.py:568
  30.4 2.1 %collective-permute-start.3 = (f32[200,128]{1,0:T(8,128)S(1)}, f32[200,128]{1,0:T(8,128)S(1)}, u32[]{:S(2)}, u32[]{:S(2)}) collective-permute-start(f32[200,128]{1,0:T(8,128)S(1)} %get-tuple-element.29), channel_id=1, source_target_pairs={{1,2},{2,1},{3,4},{4,3},{5,6},{6,5},{9,10},{10,9},{11,12},{12,11},... | collective-permute-start | bytes 307208 | tf_op jit(solution)/shard_map/ppermute | solution.py:569
  32.5 0.0 copy-start
  32.5 3.0 %shard_map.86.refs_7_ = f32[1024,128]{1,0:T(8,128)S(1)} custom-call(s32[2]{0:T(128)S(1)} %pad_add_fusion.pos.refs_0_, f32[528,128]{1,0:T(8,128)S(1)} %get-tuple-element.32.refs_1_, f32[528,128]{1,0:T(8,128)S(1)} %get-tuple-element.33.refs_2_, f32[672,128]{1,0:T(8,128)S(1)} %get-tuple-element.34.refs_3_, f32[672,128]{1,0:T(8,128)S(1)} %get-tuple-element.35.refs_4_, ...), custom_call_target="tpu_custom_call" | custom-call | flops 3000000000 | bytes 4000000 | tf_op jit(solution)/shard_map/pallas_call | solution.py:570
  35.5 0.0 collective-permute-done.2.refs_1_
  35.6 2.6 %collective-permute-done.3.refs_2_ = f32[200,128]{1,0:T(8,128)S(1)} collective-permute-done((f32[200,128]{1,0:T(8,128)S(1)}, f32[200,128]{1,0:T(8,128)S(1)}, u32[]{:S(2)}, u32[]{:S(2)}) %collective-permute-start.3) | collective-permute-done | bytes 102432 | tf_op jit(solution)/shard_map/ppermute | solution.py:569
  38.1 0.0 copy-done
  38.1 2.6 %shard_map.87 = f32[1040,128]{1,0:T(8,128)} custom-call(s32[2]{0:T(128)S(1)} %pad_add_fusion.pos.refs_0_, f32[200,128]{1,0:T(8,128)S(1)} %collective-permute-done.2.refs_1_, f32[200,128]{1,0:T(8,128)S(1)} %collective-permute-done.3.refs_2_, f32[384,128]{1,0:T(8,128)S(1)} %get-tuple-element.26.sw.refs_3_, f32[576,128]{1,0:T(8,128)S(1)} %get-tuple-element.27.sk.refs_4_, ...), custom_call_target="tpu_custom_call" | custom-call | tf_op jit(solution)/shard_map/pallas_call | solution.py:577
  (1 shorter events, 0.0 us)
Async XLA Ops:
  2.7 19.5 %collective-permute-start = (f32[816,128]{1,0:T(8,128)S(1)}, f32[816,128]{1,0:T(8,128)S(1)}, u32[]{:S(2)}, u32[]{:S(2)}) collective-permute-start(f32[816,128]{1,0:T(8,128)S(1)} %get-tuple-element.21), channel_id=1, source_target_pairs={{0,8},{8,0},{16,24},{24,16},{32,40},{40,32},{48,56},{56,48},{64,72... | collective-permute-start | bytes 1253384 | tf_op jit(solution)/shard_map/ppermute | solution.py:550
  4.6 20.7 %collective-permute-start.1 = (f32[816,128]{1,0:T(8,128)S(1)}, f32[816,128]{1,0:T(8,128)S(1)}, u32[]{:S(2)}, u32[]{:S(2)}) collective-permute-start(f32[816,128]{1,0:T(8,128)S(1)} %get-tuple-element.22), channel_id=1, source_target_pairs={{8,16},{16,8},{24,32},{32,24},{40,48},{48,40},{56,64},{64,56},{72,... | collective-permute-start | bytes 1253384 | tf_op jit(solution)/shard_map/ppermute | solution.py:549
  27.8 7.8 %collective-permute-start.2 = (f32[200,128]{1,0:T(8,128)S(1)}, f32[200,128]{1,0:T(8,128)S(1)}, u32[]{:S(2)}, u32[]{:S(2)}) collective-permute-start(f32[200,128]{1,0:T(8,128)S(1)} %get-tuple-element.28), channel_id=1, source_target_pairs={{0,1},{1,0},{2,3},{3,2},{4,5},{5,4},{6,7},{7,6},{8,9},{9,8},{10,11... | collective-permute-start | bytes 307208 | tf_op jit(solution)/shard_map/ppermute | solution.py:568
  30.4 7.8 %collective-permute-start.3 = (f32[200,128]{1,0:T(8,128)S(1)}, f32[200,128]{1,0:T(8,128)S(1)}, u32[]{:S(2)}, u32[]{:S(2)}) collective-permute-start(f32[200,128]{1,0:T(8,128)S(1)} %get-tuple-element.29), channel_id=1, source_target_pairs={{1,2},{2,1},{3,4},{4,3},{5,6},{6,5},{9,10},{10,9},{11,12},{12,11},... | collective-permute-start | bytes 307208 | tf_op jit(solution)/shard_map/ppermute | solution.py:569
  32.5 5.6 %copy-start = (f32[2,65,8,128]{3,2,1,0:T(8,128)S(1)}, f32[2,65,8,128]{3,2,1,0:T(8,128)}, u32[]{:S(2)}) copy-start(f32[2,65,8,128]{3,2,1,0:T(8,128)} %param.15) | copy-start | bytes 1597444

commit v5 on v4

--- a/solution.py
+++ b/solution.py
@@ -420,8 +420,74 @@
         stage(step)
 
 
+def fill_side(is_left, rec, sw, sk, tw, tk, mw, mk, tiles):
+    fifth = lanes() % 16
+    place = {}
+    for i, (members, width) in enumerate(GROUPS):
+        for t, k in enumerate(members):
+            place[k] = i, t, width
+    take = {}
+    for width in (5, 4):
+        start = jnp.where(is_left, 6 - width, 6)
+        take[width] = (fifth >= start) & (fifth < start + width)
+    for k in range(NQ):
+        src, index = strip_place(k, sw, sk, tw, tk)
+        here = index * 24
+        own = jnp.where(is_left, src[here : here + 8, :], src[here + 8 : here + 16, :])
+        if k in place:
+            i, t, width = place[k]
+            right_by, left_by = message_rolls(t, width)
+            by = jnp.where(is_left, -right_by % 128, -left_by % 128)
+            own = jnp.where(take[width], pltpu.roll(rec[i * 8 : i * 8 + 8, :], by, 1), own)
+        dst, start = (mw, k * tiles * 8) if k < 36 else (mk, (k - 36) * tiles * 8)
+        dst[start : start + 8, :] = own
+
+
+def side_masks(pos, columns):
+    fifth = lanes() % 16
+    west = jnp.where(pos[1] == 0, 0.0, 1.0).astype(F32)
+    east = jnp.where(pos[1] == columns - 1, 0.0, 1.0).astype(F32)
+    return (
+        jnp.where(fifth < 6, west, 1.0),
+        jnp.where((fifth >= 6) & (fifth < 12), east, 1.0),
+    )
+
+
+def diffuse_strips(tiles, masks, mw, mk, fa, fb, low, high):
+    for step in range(-1, STEPS):
+        for tile in range(tiles):
+            src, dst = (fa, fb) if step % 2 == 0 else (fb, fa)
+            put = slab(dst, tiles, tile)[1]
+            if step < 0:
+                derive(
+                    lambda n, row: at(mw, (n * 18 + row + 5) * tiles + tile),
+                    low,
+                    high,
+                    masks[tile],
+                    put,
+                )
+            else:
+                advance(
+                    STEPS - 1 - step,
+                    slab(src, tiles, tile)[0],
+                    lambda q, row: at(mk, (q * 15 + row + 4) * tiles + tile),
+                    high,
+                    masks[tile],
+                    put,
+                )
+
+
+def first_side(rows, columns, pos, rec_c, sw, sk, tw, tk, fa, mw, mk, fb):
+    low, high = ends(pos, rows)
+    odd_col = (pos[1] & 1) == 1
+    fill_side(odd_col, rec_c, sw, sk, tw, tk, mw, mk, 1)
+    left_mask, right_mask = side_masks(pos, columns)
+    diffuse_strips(1, [jnp.where(odd_col, left_mask, right_mask)], mw, mk, fa, fb, low, high)
+
+
 def finish(
-    rows, columns, pos, rec_c, rec_d, sw, sk, tw, tk, main, norm, result, mw, mk, masks, fa, fb, last_c, last_d, out, sems
+    rows, columns, pos, rec_c, rec_d, sw, sk, tw, tk, one, main, norm, result, mw, mk, fa, fb,
+    last_c, last_d, out, sems
 ):
     low, high = ends(pos, rows)
     odd_col = (pos[1] & 1) == 1
@@ -431,68 +497,30 @@
     take_left = (fifth >= 1) & (fifth <= 5)
     take_right = (fifth >= 6) & (fifth <= 10)
     take_last = (take_left & (sub == 0)) | (take_right & (sub == 1))
+    fill_side(jnp.logical_not(odd_col), rec_d, sw, sk, tw, tk, mw, mk, 2)
     for rec, unpacked in ((rec_c, last_c), (rec_d, last_d)):
         for k in range(11):
             start = NM * 8 + k // 8 * 8
             unpacked[k * 8 : k * 8 + 8, :] = roll(rec[start : start + 8, :], -16 * (k % 8))
-    take = {}
-    for width in (5, 4):
-        take[width] = (
-            (fifth >= 6 - width) & (fifth <= 5),
-            (fifth >= 6) & (fifth <= 5 + width),
-        )
-    place = {}
-    for i, (members, width) in enumerate(GROUPS):
-        for t, k in enumerate(members):
-            place[k] = i, t, width
     for k in range(NQ):
         src, index = strip_place(k, sw, sk, tw, tk)
-        here = index * 24
-        left, right = src[here : here + 8, :], src[here + 8 : here + 16, :]
-        if k in place:
-            i, t, width = place[k]
-            a = rec_c[i * 8 : i * 8 + 8, :]
-            b = rec_d[i * 8 : i * 8 + 8, :]
-            right_by, left_by = message_rolls(t, width)
-            left = jnp.where(take[width][0], roll(jnp.where(odd_col, a, b), -right_by), left)
-            right = jnp.where(take[width][1], roll(jnp.where(odd_col, b, a), -left_by), right)
+        here = index * 24 + 16
         last = jnp.where((sub == 0) == odd_col, wide(last_c, k), wide(last_d, k))
-        dst, start = (mw, k * 24) if k < 36 else (mk, (k - 36) * 24)
-        dst[start : start + 8, :] = left
-        dst[start + 8 : start + 16, :] = right
-        dst[start + 16 : start + 24, :] = jnp.where(take_last, last, src[here + 16 : here + 24, :])
-    west = jnp.where(pos[1] == 0, 0.0, 1.0).astype(F32)
-    east = jnp.where(pos[1] == columns - 1, 0.0, 1.0).astype(F32)
-    left_mask = jnp.where(fifth < 6, west, 1.0)
-    right_mask = jnp.where((fifth >= 6) & (fifth < 12), east, 1.0)
-    masks[0:8, :] = left_mask
-    masks[8:16, :] = right_mask
-    masks[16:24, :] = jnp.where(sub == 0, left_mask, jnp.where(sub == 1, right_mask, 1.0))
-    for step in range(-1, STEPS):
-        for tile in range(3):
-            mask = masks[tile * 8 : tile * 8 + 8, :]
-            src, dst = (fa, fb) if step % 2 == 0 else (fb, fa)
-            put = slab(dst, 3, tile)[1]
-            if step < 0:
-                derive(
-                    lambda n, row: at(mw, (n * 18 + row + 5) * 3 + tile), low, high, mask, put
-                )
-            else:
-                advance(
-                    STEPS - 1 - step,
-                    slab(src, 3, tile)[0],
-                    lambda q, row: at(mk, (q * 15 + row + 4) * 3 + tile),
-                    high,
-                    mask,
-                    put,
-                )
-    done = fb if STEPS % 2 == 1 else fa
+        dst, start = (mw, k * 16 + 8) if k < 36 else (mk, (k - 36) * 16 + 8)
+        dst[start : start + 8, :] = jnp.where(take_last, last, src[here : here + 8, :])
+    left_mask, right_mask = side_masks(pos, columns)
+    masks = [
+        jnp.where(odd_col, right_mask, left_mask),
+        jnp.where(sub == 0, left_mask, jnp.where(sub == 1, right_mask, 1.0)),
+    ]
+    diffuse_strips(2, masks, mw, mk, fa, fb, low, high)
     edge = (lane < 5) | (lane >= 123)
     copies = []
     for n in range(2):
         for y in range(8):
-            left, right, last = (slab(done, 3, tile)[0](n, y) for tile in range(3))
-            both = jnp.where(take_left, right, left)
+            near_side = slab(one, 1, 0)[0](n, y)
+            other, last = (slab(fa, 2, tile)[0](n, y) for tile in range(2))
+            both = jnp.where(take_left == odd_col, other, near_side)
             for tile in range(NT):
                 place = ((n * 8 + y) * NT + tile) * 8
                 value = jnp.where(edge, roll(both, -(16 * tile + 6)), main[place : place + 8, :])
@@ -574,14 +602,21 @@
         buffers((32 * 64, F32), (32 * 64, F32)),
         estimate(3_000_000_000, 4_000_000),
     )(pos, u, v, hu, hv, kt, kh)
+    (one,) = call(
+        lambda *refs: first_side(rows, columns, *refs),
+        (32 * 8,),
+        [SM] + [VM] * 5,
+        buffers((36 * 8, F32), (45 * 8, F32), (32 * 8, F32)),
+        estimate(2_000_000_000, 2_000_000),
+    )(pos, rec_c, sw, sk, tw, tk)
     (out,) = call(
         lambda *refs: finish(rows, columns, *refs),
         (2 * 65 * 8,),
-        [SM] + [VM] * 8,
-        buffers((36 * 24, F32), (45 * 24, F32), (24, F32), (32 * 24, F32), (32 * 24, F32), (88, F32), (88, F32), (1040, F32))
+        [SM] + [VM] * 9,
+        buffers((36 * 16, F32), (45 * 16, F32), (32 * 16, F32), (32 * 16, F32), (88, F32), (88, F32), (1040, F32))
         + (pltpu.SemaphoreType.DMA((2,)),),
         out_spec=HB,
-    )(pos, rec_c, rec_d, sw, sk, tw, tk, main, flat(norm_scale))
+    )(pos, rec_c, rec_d, sw, sk, tw, tk, one, main, flat(norm_scale))
     return out.reshape(norm_scale.shape)
 
 

time: 41.1 us -> 42.2 us (1.027)
  the two profiles are of different devices: /device:TPU:38 before, /device:TPU:30 now
where the time goes in v5:
time: 42.2 us; the launch traced here: 41.9 us
  starting transfers between devices  24.1 us (57%)
  Pallas kernels  15.9 us (38%)
  waiting for transfers between devices  0.96 us (2%)
  between operations  0.76 us (2%)
    ppermute x1, starting transfers between devices, on_device(): rec_b = lax.ppermute(pay_b, 'row', pairs(rows, 1))  15 us
    ppermute x1, starting transfers between devices, on_device(): rec_d = lax.ppermute(msg_d, 'col', pairs(columns, 1))  4.92 us
    pallas_call x1, Pallas kernels, on_device(): call(lambda *refs: middle(rows, *refs), (16 * 64,), [SM] + [VM] * 6, buff...  3 us
    pallas_call x1, Pallas kernels, on_device(): call(own_part, (OWN, OWN, 16 * 24, 24 * 24), [VM] * 2, work, estimate(300...  2.55 us
    pallas_call x1, Pallas kernels, on_device(): call(edges, (2 * HALO, 2 * HALO, 21 * 64 + 24, 20 * 24, 21 * 24, MSG, MSG...  2.49 us
    pallas_call x1, Pallas kernels, on_device(): call(lambda *refs: finish(rows, columns, *refs), (2 * 65 * 8,), [SM] + [V...  2.46 us
    ppermute x1, starting transfers between devices, on_device(): rec_c = lax.ppermute(msg_c, 'col', pairs(columns, 0))  2.35 us
    pallas_call x1, Pallas kernels, on_device(): call(near, (HALO, HALO), [SM, VM], work, estimate(3000000000, 2000000))  2.17 us
  transfers between devices with their start and end apart: 4, of which 1 were waited for; matrix products, arithmetic and copies ran while one was open for 0% of the time, Pallas kernels for 22%

profile of v5, /device:TPU:30, one launch (start us, length us, event | category | flops | bytes accessed | tf_op | source)
XLA Modules:
  0.0 41.9 jit_solution(15499172996734782921)
XLA Ops:
  0.7 0.1 pad_add_fusion.pos.refs_0_
  0.7 2.0 %shard_map.82 = (f32[816,128]{1,0:T(8,128)S(1)}, f32[816,128]{1,0:T(8,128)S(1)}, f32[1560,128]{1,0:T(8,128)S(1)}) custom-call(s32[2]{0:T(128)S(1)} %pad_add_fusion.pos.refs_0_, s32[1,1]{1,0:T(1,128)S(6)} %copy.9.gate, f32[32,128]{1,0:T(8,128)} %bitcast.14, s32[32,128]{1,0:T(8,128)} %bitcast.15, f32[32,128]{1,0:T(8,128)} %bitcast.16, f32[520,128]{1,0:T(8,128)} %bitcast.11, ...), custom_call_target="tpu_custom_call" | custom-call | tf_op jit(solution)/shard_map/pallas_call | solution.py:563
  2.7 1.9 %collective-permute-start = (f32[816,128]{1,0:T(8,128)S(1)}, f32[816,128]{1,0:T(8,128)S(1)}, u32[]{:S(2)}, u32[]{:S(2)}) collective-permute-start(f32[816,128]{1,0:T(8,128)S(1)} %get-tuple-element.21), channel_id=1, source_target_pairs={{0,8},{8,0},{16,24},{24,16},{32,40},{40,32},{48,56},{56,48},{64,72... | collective-permute-start | bytes 1253384 | tf_op jit(solution)/shard_map/ppermute | solution.py:578
  4.6 15.0 %collective-permute-start.1 = (f32[816,128]{1,0:T(8,128)S(1)}, f32[816,128]{1,0:T(8,128)S(1)}, u32[]{:S(2)}, u32[]{:S(2)}) collective-permute-start(f32[816,128]{1,0:T(8,128)S(1)} %get-tuple-element.22), channel_id=1, source_target_pairs={{8,16},{16,8},{24,32},{32,24},{40,48},{48,40},{56,64},{64,56},{72,... | collective-permute-start | bytes 1253384 | tf_op jit(solution)/shard_map/ppermute | solution.py:577
  19.6 2.5 %shard_map.84 = (f32[528,128]{1,0:T(8,128)S(1)}, f32[528,128]{1,0:T(8,128)S(1)}, f32[384,128]{1,0:T(8,128)S(1)}, f32[576,128]{1,0:T(8,128)S(1)}) custom-call(f32[96,128]{1,0:T(8,128)S(1)} %slice.3.obs, f32[1560,128]{1,0:T(8,128)S(1)} %get-tuple-element.25.kt.refs_5_), custom_call_target="tpu_custom_call" | custom-call | flops 3000000000 | bytes 2000000 | tf_op jit(solution)/shard_map/pallas_call | solution.py:580
  22.2 0.0 collective-permute-done.rec_a
  22.2 2.2 %shard_map.83 = (f32[336,128]{1,0:T(8,128)S(1)}, f32[336,128]{1,0:T(8,128)S(1)}) custom-call(s32[2]{0:T(128)S(1)} %pad_add_fusion.pos.refs_0_, f32[816,128]{1,0:T(8,128)S(1)} %collective-permute-done.rec_a), custom_call_target="tpu_custom_call" | custom-call | flops 3000000000 | bytes 2000000 | tf_op jit(solution)/shard_map/pallas_call | solution.py:587
  24.4 1.0 %collective-permute-done.1.rec_b = f32[816,128]{1,0:T(8,128)S(1)} collective-permute-done((f32[816,128]{1,0:T(8,128)S(1)}, f32[816,128]{1,0:T(8,128)S(1)}, u32[]{:S(2)}, u32[]{:S(2)}) %collective-permute-start.1) | collective-permute-done | bytes 417824 | tf_op jit(solution)/shard_map/ppermute | solution.py:577
  25.3 2.5 %shard_map.85 = (f32[672,128]{1,0:T(8,128)S(1)}, f32[672,128]{1,0:T(8,128)S(1)}, f32[1368,128]{1,0:T(8,128)S(1)}, f32[480,128]{1,0:T(8,128)S(1)}, f32[504,128]{1...) custom-call(s32[2]{0:T(128)S(1)} %pad_add_fusion.pos.refs_0_, ...), custom_call_target="tpu_custom_call" | custom-call | tf_op jit(solution)/shard_map/pallas_call | solution.py:590
  27.8 2.4 %collective-permute-start.2 = (f32[200,128]{1,0:T(8,128)S(1)}, f32[200,128]{1,0:T(8,128)S(1)}, u32[]{:S(2)}, u32[]{:S(2)}) collective-permute-start(f32[200,128]{1,0:T(8,128)S(1)} %get-tuple-element.28), channel_id=1, source_target_pairs={{0,1},{1,0},{2,3},{3,2},{4,5},{5,4},{6,7},{7,6},{8,9},{9,8},{10,11... | collective-permute-start | bytes 307208 | tf_op jit(solution)/shard_map/ppermute | solution.py:596
  30.2 4.9 %collective-permute-start.3 = (f32[200,128]{1,0:T(8,128)S(1)}, f32[200,128]{1,0:T(8,128)S(1)}, u32[]{:S(2)}, u32[]{:S(2)}) collective-permute-start(f32[200,128]{1,0:T(8,128)S(1)} %get-tuple-element.29), channel_id=1, source_target_pairs={{1,2},{2,1},{3,4},{4,3},{5,6},{6,5},{9,10},{10,9},{11,12},{12,11},... | collective-permute-start | bytes 307208 | tf_op jit(solution)/shard_map/ppermute | solution.py:597
  35.1 3.0 %shard_map.87.refs_8_ = f32[1024,128]{1,0:T(8,128)S(1)} custom-call(s32[2]{0:T(128)S(1)} %pad_add_fusion.pos.refs_0_, f32[528,128]{1,0:T(8,128)S(1)} %get-tuple-element.32.refs_1_, f32[528,128]{1,0:T(8,128)S(1)} %get-tuple-element.33.refs_2_, f32[672,128]{1,0:T(8,128)S(1)} %get-tuple-element.34.refs_3_, f32[672,128]{1,0:T(8,128)S(1)} %get-tuple-element.35.refs_4_, ...), custom_call_target="tpu_custom_call" | custom-call | flops 3000000000 | bytes 4000000 | tf_op jit(solution)/shard_map/pallas_call | solution.py:598
  38.1 0.0 collective-permute-done.2.refs_1_
  38.1 0.0 copy-start
  38.1 1.3 %shard_map.86.refs_7_ = f32[256,128]{1,0:T(8,128)S(1)} custom-call(s32[2]{0:T(128)S(1)} %pad_add_fusion.pos.refs_0_, f32[200,128]{1,0:T(8,128)S(1)} %collective-permute-done.2.refs_1_, f32[384,128]{1,0:T(8,128)S(1)} %get-tuple-element.26.sw.refs_2_.refs_3_, f32[576,128]{1,0:T(8,128)S(1)} %get-tuple-element.27.sk.refs_3_.refs_4_, ...), custom_call_target="tpu_custom_call" | custom-call | flops 2000000000 | bytes 2000000 | tf_op jit(solution)/shard_map/pallas_call | solution.py:605
  39.4 0.0 collective-permute-done.3.refs_2_
  39.4 0.0 copy-done
  39.4 2.5 %shard_map.88 = f32[1040,128]{1,0:T(8,128)} custom-call(s32[2]{0:T(128)S(1)} %pad_add_fusion.pos.refs_0_, f32[200,128]{1,0:T(8,128)S(1)} %collective-permute-done.2.refs_1_, f32[200,128]{1,0:T(8,128)S(1)} %collective-permute-done.3.refs_2_, f32[384,128]{1,0:T(8,128)S(1)} %get-tuple-element.26.sw.refs_2_.refs_3_, ...), custom_call_target="tpu_custom_call" | custom-call | tf_op jit(solution)/shard_map/pallas_call | solution.py:612
  (1 shorter events, 0.0 us)
Async XLA Ops:
  2.7 19.5 %collective-permute-start = (f32[816,128]{1,0:T(8,128)S(1)}, f32[816,128]{1,0:T(8,128)S(1)}, u32[]{:S(2)}, u32[]{:S(2)}) collective-permute-start(f32[816,128]{1,0:T(8,128)S(1)} %get-tuple-element.21), channel_id=1, source_target_pairs={{0,8},{8,0},{16,24},{24,16},{32,40},{40,32},{48,56},{56,48},{64,72... | collective-permute-start | bytes 1253384 | tf_op jit(solution)/shard_map/ppermute | solution.py:578
  4.6 20.7 %collective-permute-start.1 = (f32[816,128]{1,0:T(8,128)S(1)}, f32[816,128]{1,0:T(8,128)S(1)}, u32[]{:S(2)}, u32[]{:S(2)}) collective-permute-start(f32[816,128]{1,0:T(8,128)S(1)} %get-tuple-element.22), channel_id=1, source_target_pairs={{8,16},{16,8},{24,32},{32,24},{40,48},{48,40},{56,64},{64,56},{72,... | collective-permute-start | bytes 1253384 | tf_op jit(solution)/shard_map/ppermute | solution.py:577
  27.8 10.3 %collective-permute-start.2 = (f32[200,128]{1,0:T(8,128)S(1)}, f32[200,128]{1,0:T(8,128)S(1)}, u32[]{:S(2)}, u32[]{:S(2)}) collective-permute-start(f32[200,128]{1,0:T(8,128)S(1)} %get-tuple-element.28), channel_id=1, source_target_pairs={{0,1},{1,0},{2,3},{3,2},{4,5},{5,4},{6,7},{7,6},{8,9},{9,8},{10,11... | collective-permute-start | bytes 307208 | tf_op jit(solution)/shard_map/ppermute | solution.py:596
  30.2 9.3 %collective-permute-start.3 = (f32[200,128]{1,0:T(8,128)S(1)}, f32[200,128]{1,0:T(8,128)S(1)}, u32[]{:S(2)}, u32[]{:S(2)}) collective-permute-start(f32[200,128]{1,0:T(8,128)S(1)} %get-tuple-element.29), channel_id=1, source_target_pairs={{1,2},{2,1},{3,4},{4,3},{5,6},{6,5},{9,10},{10,9},{11,12},{12,11},... | collective-permute-start | bytes 307208 | tf_op jit(solution)/shard_map/ppermute | solution.py:597
  38.1 1.3 %copy-start = (f32[2,65,8,128]{3,2,1,0:T(8,128)S(1)}, f32[2,65,8,128]{3,2,1,0:T(8,128)}, u32[]{:S(2)}) copy-start(f32[2,65,8,128]{3,2,1,0:T(8,128)} %param.15) | copy-start | bytes 1597444
